TPU v7x, 32 devices: a whole 2x2x4 slice. The times are simulated.
32 devices in a mesh: dp: 8 (over z, x), fsdp: 4 (over y, core).
Axes of the slice: x: 2, y: 2, z: 4, core: 2. Of those that a mesh axis runs over, the one named last changes fastest.
Arguments:
- tokens: bfloat16 [32768, 1024], P(('dp', 'fsdp')), may hold values from -6 to 6
- lengths: int32 [32], P(('dp', 'fsdp')), may hold values from 64 to 1024, as said below
- cotangent: bfloat16 [32768, 1024], P(('dp', 'fsdp')), may hold values from -6 to 6
- w_qkv: float32 [1024, 3072], P(('dp', 'fsdp')), may hold values from -0.1875 to 0.1875
- w_out: float32 [1024, 1024], P(('dp', 'fsdp')), may hold values from -0.1875 to 0.1875
- w_fc1: float32 [1024, 4096], P(('dp', 'fsdp')), may hold values from -0.1875 to 0.1875
- w_fc2: float32 [4096, 1024], P(('dp', 'fsdp')), may hold values from -0.09375 to 0.09375
- norm_gain: float32 [3, 1024], P(None, ('dp', 'fsdp')), may hold values from 0.25 to 1.75
- norm_bias: float32 [7, 1024], P(None, ('dp', 'fsdp')), may hold values from -3 to 3
- mid_gain: float32 [4096], P(('dp', 'fsdp')), may hold values from 0.25 to 1.75
- ff_bias: float32 [2, 4096], P(None, ('dp', 'fsdp')), may hold values from -3 to 3
- head_scale: float32 [16], replicated, may hold values from 0.5 to 2
Outputs:
- out: bfloat16 [32768, 1024], P(('dp', 'fsdp'))
- grad_tokens: bfloat16 [32768, 1024], P(('dp', 'fsdp'))
- grad_qkv: float32 [1024, 3072], P(('dp', 'fsdp'))
- grad_out: float32 [1024, 1024], P(('dp', 'fsdp'))
- grad_fc1: float32 [1024, 4096], P(('dp', 'fsdp'))
- grad_fc2: float32 [4096, 1024], P(('dp', 'fsdp'))
- grad_norm_gain: float32 [3, 1024], P(None, ('dp', 'fsdp'))
- grad_norm_bias: float32 [7, 1024], P(None, ('dp', 'fsdp'))
- grad_mid_gain: float32 [4096], P(('dp', 'fsdp'))
- grad_ff_bias: float32 [2, 4096], P(None, ('dp', 'fsdp'))
- grad_head_scale: float32 [16], replicated
Inputs may be any that keep to these rules, and one draw needn't show every extreme that they name: `lengths`: every sequence's valid length; at least one sequence has exactly 1024 valid tokens and one exactly 64.
All inputs are finite; a program needn't handle non-finite values.
Results may differ from a plain program's by a relative error of at most 0.012.
Values may be sent and summed in bfloat16 or wider, within the bound.
A program may use at most 320 MiB of HBM per device.

v0:
```python
import jax
import jax.numpy as jnp
from jax import lax
from jax.sharding import PartitionSpec as P

epsilon = 1e-05
mask_fill = -1e30


def layer_norm(values):
    average = jnp.mean(values, axis=-1, keepdims=True)
    centered = values - average
    variance = jnp.mean(centered * centered, axis=-1, keepdims=True)
    return centered * lax.rsqrt(variance + epsilon)


def norm_affine(values, gain, offset):
    return layer_norm(values) * gain + offset


def gelu_exact(values):
    return jax.nn.gelu(values, approximate=False)


def to_bf16(values):
    return values.astype(jnp.bfloat16)


def plain_product(left, right):
    return jnp.dot(left, right, preferred_element_type=jnp.float32)


def row_contract(left, right):
    return lax.dot_general(
        left, right, (((0,), (0,)), ((), ())), preferred_element_type=jnp.float32
    )


def col_contract(left, right):
    return lax.dot_general(
        left, right, (((1,), (1,)), ((), ())), preferred_element_type=jnp.float32
    )


def score_block(query_block, key_rows, offset, seq_len):
    query_pos = offset + jnp.arange(query_block.shape[0], dtype=jnp.int32)
    key_pos = jnp.arange(key_rows.shape[0], dtype=jnp.int32)
    allowed = (key_pos[None, :] <= query_pos[:, None]) & (key_pos[None, :] < seq_len)
    scores = jnp.einsum("qhd,khd->hqk", query_block, key_rows, preferred_element_type=jnp.float32)
    scores = scores * query_block.shape[2] ** (-0.5)
    return jnp.where(allowed[None], scores, mask_fill)


def attend_block(query_block, key_rows, value_rows, offset, seq_len):
    scores = score_block(query_block, key_rows, offset, seq_len)
    row_max = jnp.max(scores, axis=-1, keepdims=True)
    shifted = jnp.exp(scores - row_max)
    row_sum = jnp.sum(shifted, axis=-1, keepdims=True)
    weights = to_bf16(shifted / row_sum)
    attended = jnp.einsum("hqk,khd->qhd", weights, value_rows, preferred_element_type=jnp.float32)
    return (attended, (row_max + jnp.log(row_sum))[..., 0])


def attend_sequence(query_rows, key_rows, value_rows, seq_len):
    padded = query_rows.shape[0]
    block_rows = min(512, padded)
    blocks = padded // block_rows
    query_blocks = query_rows.reshape((blocks, block_rows) + query_rows.shape[1:])
    offsets = jnp.arange(blocks, dtype=jnp.int32) * block_rows

    def one_block(pieces):
        return attend_block(pieces[0], key_rows, value_rows, pieces[1], seq_len)

    attended, log_totals = lax.map(one_block, (query_blocks, offsets))
    return (attended.reshape(query_rows.shape), log_totals)


def attend_block_back(query_block, key_rows, value_rows, grad_block, log_total, offset, seq_len):
    scores = score_block(query_block, key_rows, offset, seq_len)
    softmaxed = jnp.exp(scores - log_total[..., None])
    grad_weights = jnp.einsum(
        "qhd,khd->hqk", grad_block, value_rows, preferred_element_type=jnp.float32
    )
    grad_values = jnp.einsum(
        "hqk,qhd->khd", to_bf16(softmaxed), grad_block, preferred_element_type=jnp.float32
    )
    centered = grad_weights - jnp.sum(softmaxed * grad_weights, axis=-1, keepdims=True)
    grad_scores = to_bf16(softmaxed * centered)
    scaling = query_block.shape[2] ** (-0.5)
    grad_queries = (
        jnp.einsum("hqk,khd->qhd", grad_scores, key_rows, preferred_element_type=jnp.float32)
        * scaling
    )
    grad_keys = (
        jnp.einsum("hqk,qhd->khd", grad_scores, query_block, preferred_element_type=jnp.float32)
        * scaling
    )
    return (grad_queries, grad_keys, grad_values)


def attend_sequence_back(query_rows, key_rows, value_rows, grad_rows, log_totals, seq_len):
    padded = query_rows.shape[0]
    block_rows = min(512, padded)
    blocks = padded // block_rows
    query_blocks = query_rows.reshape((blocks, block_rows) + query_rows.shape[1:])
    grad_blocks = grad_rows.reshape((blocks, block_rows) + grad_rows.shape[1:])
    offsets = jnp.arange(blocks, dtype=jnp.int32) * block_rows

    def step_block(totals, pieces):
        grad_queries, grad_keys, grad_values = attend_block_back(
            pieces[0], key_rows, value_rows, pieces[1], pieces[2], pieces[3], seq_len
        )
        return ((totals[0] + grad_keys, totals[1] + grad_values), grad_queries)

    zeros_kv = jnp.zeros(key_rows.shape, jnp.float32)
    (grad_keys, grad_values), grad_queries = lax.scan(
        step_block, (zeros_kv, zeros_kv), (query_blocks, grad_blocks, log_totals, offsets)
    )
    return (grad_queries.reshape(query_rows.shape), grad_keys, grad_values)


def shards(
    tokens,
    lengths,
    cotangent,
    w_qkv,
    w_out,
    w_fc1,
    w_fc2,
    norm_gain,
    norm_bias,
    mid_gain,
    ff_bias,
    head_scale,
):
    full_qkv, full_out, full_fc1, full_fc2, gain_copy, bias_copy, mid_copy, ff_copy = (
        lax.all_gather(to_bf16(w_qkv), ("dp", "fsdp"), axis=0, tiled=True),
        lax.all_gather(to_bf16(w_out), ("dp", "fsdp"), axis=0, tiled=True),
        lax.all_gather(to_bf16(w_fc1), ("dp", "fsdp"), axis=0, tiled=True),
        lax.all_gather(to_bf16(w_fc2), ("dp", "fsdp"), axis=0, tiled=True),
        lax.all_gather(to_bf16(norm_gain), ("dp", "fsdp"), axis=1, tiled=True),
        lax.all_gather(to_bf16(norm_bias), ("dp", "fsdp"), axis=1, tiled=True),
        lax.all_gather(to_bf16(mid_gain), ("dp", "fsdp"), axis=0, tiled=True),
        lax.all_gather(to_bf16(ff_bias), ("dp", "fsdp"), axis=1, tiled=True),
    )
    gains = gain_copy.astype(jnp.float32)
    biases = bias_copy.astype(jnp.float32)
    mid_gains = mid_copy.astype(jnp.float32)
    ff_biases = ff_copy.astype(jnp.float32)
    seq_total = lengths.shape[0]
    row_total = tokens.shape[0]
    padded = row_total // seq_total
    width = tokens.shape[1]
    heads = head_scale.shape[0]
    head_dim = width // heads
    seq_shape = (seq_total, padded, heads, head_dim)
    x_in = tokens.astype(jnp.float32)
    normed_in = to_bf16(norm_affine(x_in, gains[0], biases[0]))
    projected = plain_product(normed_in, full_qkv)
    queries = to_bf16(projected[:, :width] + biases[1])
    key_rows = to_bf16(projected[:, width : 2 * width])
    value_rows = to_bf16(projected[:, 2 * width :] + biases[2])

    def forward_sequence(pieces):
        return attend_sequence(pieces[0], pieces[1], pieces[2], pieces[3])

    attended, log_totals = lax.map(
        forward_sequence,
        (
            queries.reshape(seq_shape),
            key_rows.reshape(seq_shape),
            value_rows.reshape(seq_shape),
            lengths,
        ),
    )
    attended = attended.reshape(row_total, heads, head_dim)
    mixed = to_bf16((attended * head_scale[None, :, None]).reshape(row_total, width))
    projection = plain_product(mixed, full_out) + biases[3]
    residual = x_in + norm_affine(projection, gains[1], biases[4])
    normed_ff = to_bf16(norm_affine(residual, gains[2], biases[5]))
    pre_act = plain_product(normed_ff, full_fc1) + ff_biases[0]
    activated = gelu_exact(pre_act)
    normed_mid = to_bf16(norm_affine(activated, mid_gains, ff_biases[1]))
    result = residual + (plain_product(normed_mid, full_fc2) + biases[6])
    positions = jnp.arange(padded, dtype=jnp.int32)
    valid = (positions[None, :] < lengths[:, None]).astype(jnp.float32).reshape(row_total, 1)
    grad_result = cotangent.astype(jnp.float32) * valid
    back_qkv, back_out, back_fc1, back_fc2 = (
        lax.all_gather(to_bf16(w_qkv), ("dp", "fsdp"), axis=0, tiled=True),
        lax.all_gather(to_bf16(w_out), ("dp", "fsdp"), axis=0, tiled=True),
        lax.all_gather(to_bf16(w_fc1), ("dp", "fsdp"), axis=0, tiled=True),
        lax.all_gather(to_bf16(w_fc2), ("dp", "fsdp"), axis=0, tiled=True),
    )
    grad_branch = to_bf16(grad_result)
    grad_fc2 = row_contract(normed_mid, grad_branch)
    grad_bias_fc2 = jnp.sum(grad_branch.astype(jnp.float32), axis=0)
    grad_mid = col_contract(grad_branch, back_fc2)
    _, mid_pull = jax.vjp(norm_affine, activated, mid_gains, ff_biases[1])
    grad_activated, grad_mid_gain, grad_mid_bias = mid_pull(grad_mid)
    _, gelu_pull = jax.vjp(gelu_exact, pre_act)
    grad_pre = to_bf16(gelu_pull(grad_activated)[0])
    grad_fc1 = row_contract(normed_ff, grad_pre)
    grad_bias_fc1 = jnp.sum(grad_pre.astype(jnp.float32), axis=0)
    grad_ff_biases = jnp.stack((grad_bias_fc1, grad_mid_bias))
    grad_normed_ff = col_contract(grad_pre, back_fc1)
    _, ff_pull = jax.vjp(norm_affine, residual, gains[2], biases[5])
    grad_res_part, grad_gain_ff, grad_bias_ff = ff_pull(grad_normed_ff)
    grad_residual = grad_result + grad_res_part
    _, post_pull = jax.vjp(norm_affine, projection, gains[1], biases[4])
    grad_projection, grad_gain_post, grad_bias_post = post_pull(grad_residual)
    grad_projection = to_bf16(grad_projection)
    grad_out_w = row_contract(mixed, grad_projection)
    grad_bias_out = jnp.sum(grad_projection.astype(jnp.float32), axis=0)
    grad_mixed = col_contract(grad_projection, back_out).reshape(row_total, heads, head_dim)
    grad_scale_local = jnp.sum(grad_mixed * attended, axis=(0, 2))
    grad_attended = to_bf16(grad_mixed * head_scale[None, :, None])

    def backward_sequence(pieces):
        return attend_sequence_back(
            pieces[0], pieces[1], pieces[2], pieces[3], pieces[4], pieces[5]
        )

    grad_queries, grad_keys, grad_values = lax.map(
        backward_sequence,
        (
            queries.reshape(seq_shape),
            key_rows.reshape(seq_shape),
            value_rows.reshape(seq_shape),
            grad_attended.reshape(seq_shape),
            log_totals,
            lengths,
        ),
    )
    grad_projected = to_bf16(
        jnp.concatenate(
            (
                grad_queries.reshape(row_total, width),
                grad_keys.reshape(row_total, width),
                grad_values.reshape(row_total, width),
            ),
            axis=1,
        )
    )
    grad_qkv = row_contract(normed_in, grad_projected)
    grad_bias_q = jnp.sum(grad_projected[:, :width].astype(jnp.float32), axis=0)
    grad_bias_v = jnp.sum(grad_projected[:, 2 * width :].astype(jnp.float32), axis=0)
    grad_normed_in = col_contract(grad_projected, back_qkv)
    _, in_pull = jax.vjp(norm_affine, x_in, gains[0], biases[0])
    grad_x_part, grad_gain_in, grad_bias_in = in_pull(grad_normed_in)
    grad_tokens = (grad_residual + grad_x_part).astype(jnp.bfloat16)
    grad_gains = jnp.stack((grad_gain_in, grad_gain_post, grad_gain_ff))
    grad_biases = jnp.stack(
        (
            grad_bias_in,
            grad_bias_q,
            grad_bias_v,
            grad_bias_out,
            grad_bias_post,
            grad_bias_ff,
            grad_bias_fc2,
        )
    )
    summed = (
        lax.psum_scatter(grad_qkv, ("dp", "fsdp"), scatter_dimension=0, tiled=True),
        lax.psum_scatter(grad_out_w, ("dp", "fsdp"), scatter_dimension=0, tiled=True),
        lax.psum_scatter(grad_fc1, ("dp", "fsdp"), scatter_dimension=0, tiled=True),
        lax.psum_scatter(grad_fc2, ("dp", "fsdp"), scatter_dimension=0, tiled=True),
        lax.psum_scatter(grad_gains, ("dp", "fsdp"), scatter_dimension=1, tiled=True),
        lax.psum_scatter(grad_biases, ("dp", "fsdp"), scatter_dimension=1, tiled=True),
        lax.psum_scatter(grad_mid_gain, ("dp", "fsdp"), scatter_dimension=0, tiled=True),
        lax.psum_scatter(grad_ff_biases, ("dp", "fsdp"), scatter_dimension=1, tiled=True),
    )
    grad_scale = lax.psum(grad_scale_local, ("dp", "fsdp"))
    return (
        result.astype(jnp.bfloat16),
        grad_tokens,
        summed[0],
        summed[1],
        summed[2],
        summed[3],
        summed[4],
        summed[5],
        summed[6],
        summed[7],
        grad_scale,
    )


def solution(mesh):
    placed = (
        P(("dp", "fsdp"), None),
        P(("dp", "fsdp")),
        P(("dp", "fsdp"), None),
        P(("dp", "fsdp"), None),
        P(("dp", "fsdp"), None),
        P(("dp", "fsdp"), None),
        P(("dp", "fsdp"), None),
        P(None, ("dp", "fsdp")),
        P(None, ("dp", "fsdp")),
        P(("dp", "fsdp")),
        P(None, ("dp", "fsdp")),
        P(),
    )
    return jax.shard_map(
        shards,
        mesh=mesh,
        in_specs=placed,
        out_specs=(
            P(("dp", "fsdp"), None),
            P(("dp", "fsdp"), None),
            P(("dp", "fsdp"), None),
            P(("dp", "fsdp"), None),
            P(("dp", "fsdp"), None),
            P(("dp", "fsdp"), None),
            P(None, ("dp", "fsdp")),
            P(None, ("dp", "fsdp")),
            P(("dp", "fsdp")),
            P(None, ("dp", "fsdp")),
            P(),
        ),
        check_vma=False,
    )
```

profile of v0, /device:TPU:0, one launch (start us, length us, event | category | flops | bytes accessed | tf_op | source)
XLA Modules:
  0.0 1925.9 jit_solution(8272963947455519974)
XLA Ops:
  19.7 43.0 %all_gather.33 = bf16[2,4096]{1,0:T(2,128)(2,1)S(1)} all-gather(bf16[2,128]{1,0:T(2,128)(2,1)S(1)} %convert_element_type.131), channel_id=1, replica_groups=mesh['dp'=8,'fsdp'=4] {'dp','fsdp'}, dimensions={1}, use_global_device_ids=true | all-gather | bytes 16896 | tf_op jit(solution)/shard_map/all_gather | solution.py:144
  62.7 36.6 %all-gather.2 = bf16[32,1,128]{2,1,0:T(2,128)(2,1)S(1)} all-gather(bf16[1,1,128]{2,1,0:T(2,128)(2,1)S(1)} %convert_bitcast_fusion.2), channel_id=1, replica_groups=mesh['dp'=8,'fsdp'=4] {'dp','fsdp'}, dimensions={0}, use_global_device_ids=true | all-gather | bytes 8448 | tf_op jit(solution)/shard_map/all_gather | solution.py:143
  100.6 38.0 %all-gather = bf16[32,32,3]{1,2,0:T(4,128)(2,1)S(1)} all-gather(bf16[1,32,3]{1,2,0:T(4,128)(2,1)S(1)} %convert_bitcast_fusion.1), channel_id=1, replica_groups=mesh['dp'=8,'fsdp'=4] {'dp','fsdp'}, dimensions={0}, use_global_device_ids=true | all-gather | bytes 6336 | tf_op jit(solution)/shard_map/all_gather | solution.py:141
  139.3 37.2 %all-gather.1 = bf16[32,32,7]{1,2,0:T(8,128)(2,1)S(1)} all-gather(bf16[1,32,7]{1,2,0:T(8,128)(2,1)S(1)} %convert_bitcast_fusion), channel_id=1, replica_groups=mesh['dp'=8,'fsdp'=4] {'dp','fsdp'}, dimensions={0}, use_global_device_ids=true | all-gather | bytes 14784 | tf_op jit(solution)/shard_map/all_gather | solution.py:142
  181.7 3.9 copy.112
  185.6 9.3 fusion.73
  198.6 3.9 copy.108
  205.1 6.4 reshape.368
  211.5 5.4 copy.109
  217.0 176.3 %while.47 = (s32[]{:T(128)}, f32[2,512,16,64]{1,0,3,2:T(2,128)}, f32[2,16,512]{2,1,0:T(8,128)S(1)}, s32[2]{0:T(128)S(1)}, s32[]{:T(128)}, /*index=5*/bf16[2,512,...) while((s32[]{:T(128)}, f32[2,512,16,64]{1,0,3,2:T(2,128)}, ...), condition=%wide.region_5.6_spmd, body=%wide.region_2.5_spmd.sunk | while | flops 2249188864 | bytes 118757512 | solution.py:74
  219.5 16.1 fusion.129
  235.6 14.9 fusion.130
  250.5 14.7 fusion.131
  267.5 38.1 %dynamic_update_slice.30 = f32[2,512,16,64]{1,0,3,2:T(2,128)} dynamic-update-slice(f32[2,512,16,64]{1,0,3,2:T(2,128)} %get-tuple-element.588, f32[1,512,16,64]{1,0,3,2:T(1,128)S(1)} %copy.171, s32[]{:T(128)S(6)} %copy.178, s32[]{:T(128)} %constant.75.clone.1..sunk, s32[]{:T(128)} %constant.75.clone.1..sunk, s32[]{:T(128)} %constant.75.clone.1..sunk) | dynamic-update-slice | bytes 4194308 | tf_op jit(solution)/shard_map/while/body/eval_jaxpr/while/body/jit(dynamic_update_index_in_dim)/dynamic_update_slice | solution.py:74
  307.9 15.6 fusion.129
  323.5 14.9 fusion.130
  338.4 14.6 fusion.131
  355.2 38.0 %dynamic_update_slice.30 = f32[2,512,16,64]{1,0,3,2:T(2,128)} dynamic-update-slice(f32[2,512,16,64]{1,0,3,2:T(2,128)} %get-tuple-element.588, f32[1,512,16,64]{1,0,3,2:T(1,128)S(1)} %copy.171, s32[]{:T(128)S(6)} %copy.178, s32[]{:T(128)} %constant.75.clone.1..sunk, s32[]{:T(128)} %constant.75.clone.1..sunk, s32[]{:T(128)} %constant.75.clone.1..sunk) | dynamic-update-slice | bytes 4194308 | tf_op jit(solution)/shard_map/while/body/eval_jaxpr/while/body/jit(dynamic_update_index_in_dim)/dynamic_update_slice | solution.py:74
  393.3 5.2 copy.166
  398.4 5.8 copy.121
  404.3 5.3 add_reduce_fusion
  418.2 49.9 %fusion.78 = (f32[1024]{0:T(1024)S(1)}, f32[1024,4096]{1,0:T(8,128)}, f32[1024,4096]{1,0:T(8,128)}, f32[1024,4096]{1,0:T(8,128)}) fusion(f32[4096]{0:T(1024)S(1)} %bitcast.198, bf16[1024,4096]{1,0:T(8,128)(2,1)} %all-gather.12.cloned.1.call-done, bf16[1024,1024]{0,1:T(8,128)(2,1)} %add_convert_fusion.7.clone.4), kind=kOutput, calls=%fused_computation.161 | convolution fusion | flops 8866757632 | bytes 60837888 | tf_op jit(solution)/shard_map/dot_general | solution.py:30
  468.0 22.4 %multiply_reduce_fusion.2 = (f32[1024]{0:T(1024)S(1)}, f32[1024]{0:T(1024)S(1)}, f32[4096]{0:T(1024)}, f32[1024,4096]{1,0:T(8,128)}) fusion(f32[1024,4096]{1,0:T(8,128)} %get-tuple-element.417, f32[4096]{0:T(1024)S(1)} %bitcast.179, f32[1024]{0:T(1024)S(1)} %broadcast_multiply_fusion, bf16[4096,1024]{1,0:T(8,128)(2,1)} %all-gather.14.cloned.1.call-done, ...), kind=kOutput, calls=%fused_computation.54 | convolution fusion | flops 8622434304 | bytes 44089344 | tf_op jit(solution)/shard_map/dot_general | solution.py:40
  490.5 13.4 multiply_reduce_fusion.1
  503.8 28.4 %convert_reduce_fusion = (f32[4096]{0:T(1024)}, bf16[1024,4096]{1,0:T(8,128)(2,1)S(1)}, bf16[1024,4096]{1,0:T(8,128)(2,1)}) fusion(f32[1024,4096]{1,0:T(8,128)} %get-tuple-element.418, f32[1024]{0:T(1024)S(1)} %negate_multiply_fusion.4, f32[1024]{0:T(1024)S(1)} %get-tuple-element.441, f32[1024,4096]{1,0:T(8,128)} %get-tuple-element.417, ...), kind=kLoop, calls=%fused_computation.51 | loop fusion | flops 117436416 | bytes 83968000 | tf_op jit(solution)/shard_map/reduce_sum | solution.py:203
  532.3 16.2 fusion.85
  548.5 5.4 copy.113
  553.9 4.2 multiply_reduce_fusion.8
  562.7 5.2 multiply_reduce_fusion.6
  573.5 4.9 multiply_reduce_fusion.4
  578.4 5.4 copy.114
  583.8 6.6 reshape.342
  590.4 4.0 multiply_convert_fusion.1
  596.2 221.3 %while.48 = (s32[]{:T(128)}, f32[1024,16,64]{0,2,1:T(8,128)}, f32[1024,16,64]{0,2,1:T(8,128)}, bf16[2,512,16,64]{1,3,2,0:T(8,128)(2,1)}, bf16[2,512,16,64]{1,3,2...) while((s32[]{:T(128)}, f32[1024,16,64]{0,2,1:T(8,128)}, ...), condition=%wide.region_20.21_spmd.clone, body=%wide.region_18.20_spmd.clone.sunk | while | flops 5501347328 | bytes 350460096 | solution.py:116
  598.7 17.5 fusion.141
  616.2 17.6 bitcast_add_fusion.5
  633.8 25.9 %multiply_reduce_fusion.12 = (f32[16,512]{1,0:T(8,128)S(1)}, f32[16,512,1024]{2,1,0:T(8,128)}) fusion(f32[16,512,1024]{2,1,0:T(8,128)} %fusion.141, f32[16,512]{1,0:T(8,128)S(1)} %dynamic-slice_bitcast_fusion.2, pred[512,1024]{1,0:T(8,128)(4,1)S(1)} %fusion.142, bf16[1024,16,64]{0,2,1:T(8,128)(2,1)} %get-tuple-element.643, ...), kind=kOutput, calls=%fused_computation.19.clone.1 | convolution fusion | flops 1115676672 | bytes 70844416 | tf_op jit(solution)/shard_map/while/body/eval_jaxpr/while/body/eval_jaxpr/qhd,khd->hqk/dot_general | solution.py:81
  659.8 27.8 %multiply_convert_fusion.6 = bf16[16,512,1024]{2,1,0:T(8,128)(2,1)} fusion(f32[16,512,1024]{2,1,0:T(8,128)} %get-tuple-element.575, f32[16,512,1024]{2,1,0:T(8,128)} %fusion.141, f32[16,512]{1,0:T(8,128)S(1)} %get-tuple-element.576, f32[16,512]{1,0:T(8,128)S(1)} %dynamic-slice_bitcast_fusion.2, pred[512,1024]{1,0:T(8,128)(4,1)S(1)} %fusion.142), kind=kLoop, calls=%fused_computation.18.clone.1 | loop fusion | flops 50331648 | bytes 84475904 | tf_op jit(solution)/shard_map/while/body/eval_jaxpr/while/body/eval_jaxpr/convert_element_type | solution.py:26
  687.5 10.3 bitcast_dynamic-update-slice_fusion.5
  699.1 6.4 bitcast_add_fusion.4
  707.8 17.5 fusion.141
  725.4 18.8 bitcast_add_fusion.5
  744.2 25.9 %multiply_reduce_fusion.12 = (f32[16,512]{1,0:T(8,128)S(1)}, f32[16,512,1024]{2,1,0:T(8,128)}) fusion(f32[16,512,1024]{2,1,0:T(8,128)} %fusion.141, f32[16,512]{1,0:T(8,128)S(1)} %dynamic-slice_bitcast_fusion.2, pred[512,1024]{1,0:T(8,128)(4,1)S(1)} %fusion.142, bf16[1024,16,64]{0,2,1:T(8,128)(2,1)} %get-tuple-element.643, ...), kind=kOutput, calls=%fused_computation.19.clone.1 | convolution fusion | flops 1115676672 | bytes 70844416 | tf_op jit(solution)/shard_map/while/body/eval_jaxpr/while/body/eval_jaxpr/qhd,khd->hqk/dot_general | solution.py:81
  770.1 27.8 %multiply_convert_fusion.6 = bf16[16,512,1024]{2,1,0:T(8,128)(2,1)} fusion(f32[16,512,1024]{2,1,0:T(8,128)} %get-tuple-element.575, f32[16,512,1024]{2,1,0:T(8,128)} %fusion.141, f32[16,512]{1,0:T(8,128)S(1)} %get-tuple-element.576, f32[16,512]{1,0:T(8,128)S(1)} %dynamic-slice_bitcast_fusion.2, pred[512,1024]{1,0:T(8,128)(4,1)S(1)} %fusion.142), kind=kLoop, calls=%fused_computation.18.clone.1 | loop fusion | flops 50331648 | bytes 84475904 | tf_op jit(solution)/shard_map/while/body/eval_jaxpr/while/body/eval_jaxpr/convert_element_type | solution.py:26
  797.9 10.3 bitcast_dynamic-update-slice_fusion.5
  809.4 7.7 bitcast_add_fusion.4
  817.5 3.9 copy.117
  828.3 8.4 fusion.84
  836.7 5.5 copy.118
  854.6 7.2 fusion.69
  862.5 14.2 fusion.55
  877.4 16.6 fusion.75
  894.7 16.2 fusion.57
  911.6 15.4 add_convert_fusion.4
  927.0 3.9 copy.122
  931.0 6.2 add_convert_fusion.2
  937.2 4.0 copy.123
  941.2 37.3 %all-reduce.1 = (f32[4096]{0:T(1024)S(1)}, f32[16]{0:T(128)}) all-reduce(f32[4096]{0:T(1024)S(1)} %copy-done.43, f32[16]{0:T(128)S(1)} %reduce_sum.347), channel_id=8, replica_groups=mesh['dp'=8,'fsdp'=4] {'dp','fsdp'}, use_global_device_ids=true, to_apply=%region_40.41.clone | all-reduce | flops 4112 | bytes 32896
  981.8 130.8 %reduce-scatter.24.cloned.1.call-done = f32[32,7]{1,0:T(8,128)} async-done(((f32[1024,7]{1,0:T(8,128)}), f32[32,7]{1,0:T(8,128)}) %reduce-scatter.24.cloned.1.call-update) | async-done | bytes 912
  1114.0 133.6 %reduce-scatter.26.cloned.1.call-done = f32[128,2]{1,0:T(8,128)} async-done(((f32[4096,2]{1,0:T(8,128)}), f32[128,2]{1,0:T(8,128)}) %reduce-scatter.26.cloned.1.call-update) | async-done | bytes 1040
  1249.2 138.9 %reduce-scatter.16.cloned.1.call-done = f32[32,1024]{1,0:T(8,128)} async-done(((f32[1024,1024]{1,0:T(8,128)}), f32[32,1024]{1,0:T(8,128)}) %reduce-scatter.16.cloned.1.call-update) | async-done | bytes 131088 | tf_op jit(solution)/shard_map/reduce_scatter | solution.py:265
  1388.0 158.9 %reduce-scatter.14.cloned.1.call-done = f32[32,3072]{1,0:T(8,128)} async-done(((f32[1024,3072]{1,0:T(8,128)}), f32[32,3072]{1,0:T(8,128)}) %reduce-scatter.14.cloned.1.call-update) | async-done | bytes 393232 | tf_op jit(solution)/shard_map/reduce_scatter | solution.py:264
  1546.9 184.8 %reduce-scatter.18.cloned.1.call-done = f32[32,4096]{1,0:T(8,128)} async-done(((f32[1024,4096]{1,0:T(8,128)}), f32[32,4096]{1,0:T(8,128)}) %reduce-scatter.18.cloned.1.call-update) | async-done | bytes 524304 | tf_op jit(solution)/shard_map/reduce_scatter | solution.py:266
  1731.7 187.5 %reduce-scatter.20.cloned.1.call-done = f32[128,1024]{1,0:T(8,128)} async-done(((f32[4096,1024]{1,0:T(8,128)}), f32[128,1024]{1,0:T(8,128)}) %reduce-scatter.20.cloned.1.call-update) | async-done | bytes 524304 | tf_op jit(solution)/shard_map/reduce_scatter | solution.py:267
  (283 shorter events, 89.3 us)
Async XLA Ops:
  7.2 178.4 %all-gather.8.cloned.1.call-start = ((), (), s32[]{:S(2)}) async-start(), calls=%async_computation.7 | async-start | bytes 6488064 | tf_op jit(solution)/shard_map/all_gather | solution.py:137
  8.9 395.3 %all-gather.10.cloned.1.call-start = ((), (), s32[]{:S(2)}) async-start(), calls=%async_computation.8 | async-start | bytes 2162688 | tf_op jit(solution)/shard_map/all_gather | solution.py:138
  10.6 407.6 %all-gather.12.cloned.1.call-start = ((), (), s32[]{:S(2)}) async-start(), calls=%async_computation.9 | async-start | bytes 8650752 | tf_op jit(solution)/shard_map/all_gather | solution.py:139
  12.4 455.6 %all-gather.14.cloned.1.call-start = ((), (), s32[]{:S(2)}) async-start(), calls=%async_computation.10 | async-start | bytes 8650752 | tf_op jit(solution)/shard_map/all_gather | solution.py:140
  14.3 966.2 %reduce-scatter.22.cloned.1.call-start = ((), (), s32[]{:S(2)}) async-start(), calls=%async_computation.15 | async-start | bytes 540672
  139.3 46.3 %copy-start.47 = (f32[1,1024]{1,0:T(1,128)}, f32[1,1024]{1,0:T(1,128)S(1)}, u32[]{:S(2)}) copy-start(f32[1,1024]{1,0:T(1,128)S(1)} %get-tuple-element.440) | copy-start | bytes 12292
  177.2 8.4 copy-start.69
  180.1 5.6 copy-start.4
  180.5 14.5 copy-start.34
  181.7 13.3 copy-start.49
  393.2 5.2 copy-start.21
  393.2 5.2 copy-start.78
  398.4 5.8 copy-start.30
  398.4 5.9 copy-start.71
  409.6 4.5 copy-start.8
  409.7 3.1 copy-start.5
  409.7 4.5 copy-start.32
  410.3 3.9 copy-start.53
  410.4 3.9 copy-start.39
  418.1 49.9 %copy-start.13 = (bf16[1024,1024]{0,1:T(8,128)(2,1)S(1)}, bf16[1024,1024]{0,1:T(8,128)(2,1)}, u32[]{:S(2)}) copy-start(bf16[1024,1024]{0,1:T(8,128)(2,1)} %copy.112) | copy-start | bytes 6291460
  418.2 49.9 %copy-start.26 = (f32[32,1,128]{2,1,0:T(1,128)S(1)}, f32[32,1,128]{2,1,0:T(1,128)}, u32[]{:S(2)}) copy-start(f32[32,1,128]{2,1,0:T(1,128)} %convert_element_type.152) | copy-start | bytes 49156
  418.2 49.9 %copy-start.62 = (f32[1024]{0:T(1024)S(1)}, f32[1024]{0:T(1024)}, u32[]{:S(2)}) copy-start(f32[1024]{0:T(1024)} %fusion.62) | copy-start | bytes 12292
  490.5 13.4 copy-start.45
  532.3 16.2 copy-start.12
  548.5 5.4 copy-start.24
  548.5 5.4 copy-start.28
  553.9 4.3 copy-start.56
  553.9 4.6 copy-start.3
  553.9 5.9 copy-start.10
  553.9 5.9 copy-start.37
  562.7 5.2 copy-start.54
  569.9 3.6 copy-start.77
  570.9 7.5 copy-start.19
  583.8 6.6 copy-start.75
  590.4 5.8 copy-start.22
  590.4 5.8 copy-start.79
  687.5 11.5 copy-start
  797.9 11.5 copy-start
  817.5 4.5 copy-start.1
  822.0 4.0 copy-start.15
  822.0 3.7 copy-start.16
  822.3 14.4 copy-start.18
  822.3 6.0 copy-start.76
  826.0 10.7 copy-start.20
  836.7 5.6 copy-start.6
  836.7 5.6 copy-start.35
  836.7 5.5 copy-start.48
  842.3 3.5 copy-start.7
  842.3 3.4 copy-start.50
  845.7 5.3 copy-start.64
  845.7 5.3 copy-start.65
  845.7 5.3 copy-start.66
  845.7 5.3 copy-start.74
  845.7 6.5 copy-start.44
  845.8 6.5 copy-start.67
  848.0 6.6 copy-start.72
  849.0 263.6 %reduce-scatter.24.cloned.1.call-start = ((), (), s32[]{:S(2)}) async-start(), calls=%async_computation.16 | async-start | bytes 540672
  852.2 395.5 %reduce-scatter.26.cloned.1.call-start = ((), (), s32[]{:S(2)}) async-start(), calls=%async_computation.17 | async-start | bytes 2162688
  854.4 533.6 %reduce-scatter.16.cloned.1.call-start = ((), (), s32[]{:S(2)}) async-start(), calls=%async_computation.12 | async-start | bytes 4325376 | tf_op jit(solution)/shard_map/reduce_scatter | solution.py:265
  861.9 685.0 %reduce-scatter.14.cloned.1.call-start = ((), (), s32[]{:S(2)}) async-start(), calls=%async_computation.11 | async-start | bytes 12976128 | tf_op jit(solution)/shard_map/reduce_scatter | solution.py:264
  876.7 855.0 %reduce-scatter.18.cloned.1.call-start = ((), (), s32[]{:S(2)}) async-start(), calls=%async_computation.13 | async-start | bytes 17301504 | tf_op jit(solution)/shard_map/reduce_scatter | solution.py:266
  894.1 1025.1 %reduce-scatter.20.cloned.1.call-start = ((), (), s32[]{:S(2)}) async-start(), calls=%async_computation.14 | async-start | bytes 17301504 | tf_op jit(solution)/shard_map/reduce_scatter | solution.py:267
  927.0 3.9 copy-start.73
  937.2 4.1 copy-start.43
  (28 other events, 53.5 us)
Sparse Core Ops, SparseCore 0:
  11.5 72.3 all-gather.7
  87.3 54.8 all-gather.9
  145.7 76.0 all-gather.11
  225.1 76.0 all-gather.13
  849.2 131.2 reduce-scatter.21
  982.6 129.9 reduce-scatter.23
  1114.9 132.7 reduce-scatter.25
  1250.6 137.3 reduce-scatter.15
  1395.6 151.2 reduce-scatter.13
  1549.6 182.0 reduce-scatter.17
  1734.6 184.5 reduce-scatter.19
where the time goes:
time: 1940 us; the launch traced here: 1930 us
  waiting for transfers between devices  936 us (48%)
  matrix products  405 us (21%)
  blocking collectives  192 us (10%)
  local copies, waits for them, and re-layouts  189 us (10%)
  other arithmetic  186 us (10%)
    unnamed x14, waiting for transfers between devices  266 us
    reduce_scatter x1, waiting for transfers between devices, shards(): lax.psum_scatter(grad_fc2, ('dp', 'fsdp'), scatter_dimension=0, tiled=True)  187 us
    reduce_scatter x1, waiting for transfers between devices, shards(): lax.psum_scatter(grad_fc1, ('dp', 'fsdp'), scatter_dimension=0, tiled=True)  185 us
    reduce_scatter x1, waiting for transfers between devices, shards(): lax.psum_scatter(grad_qkv, ('dp', 'fsdp'), scatter_dimension=0, tiled=True)  159 us
    reduce_scatter x1, waiting for transfers between devices, shards(): lax.psum_scatter(grad_out_w, ('dp', 'fsdp'), scatter_dimension=0, tiled=T...  139 us
    dynamic_update_slice x4, local copies, waits for them, and re-layouts, attend_sequence(): attended, log_totals = lax.map(one_block, (query_blocks, offsets))  80.5 us
    dot_general x4, matrix products, plain_product(): return jnp.dot(left, right, preferred_element_type=jnp.float32)  79.8 us
    convert_element_type x9, other arithmetic, to_bf16(): return values.astype(jnp.bfloat16)  70.3 us
  transfers between devices with their start and end apart: 11, of which 7 were waited for; matrix products, arithmetic and copies ran while one was open for 20% of the time, Pallas kernels for 0%

commit v1 on v0

--- a/solution.py
+++ b/solution.py
@@ -1,10 +1,347 @@
+import functools
+
 import jax
 import jax.numpy as jnp
 from jax import lax
+from jax.experimental import pallas as pl
+from jax.experimental.pallas import tpu as pltpu
 from jax.sharding import PartitionSpec as P
 
 epsilon = 1e-05
 mask_fill = -1e30
+MESH = pl.DeviceIdType.MESH
+ORDERS = ((1, 2, 0), (2, 1, 0), (0, 1, 2), (0, 2, 1))
+
+
+def digits_of(mesh):
+    dp, fsdp = mesh.shape["dp"], mesh.shape["fsdp"]
+    minor = 2 if dp <= 8 else 8
+    return (dp // minor, minor, fsdp // 2, 2)
+
+
+class Place:
+    def __init__(self, digits):
+        self.digits = digits
+        dp, fs = lax.axis_index("dp"), lax.axis_index("fsdp")
+        self.at = (dp // digits[1], dp % digits[1], fs // digits[3], fs % digits[3])
+
+    def digit(self, axis, shift):
+        n = self.digits[axis]
+        return (self.at[axis] + shift + n) % n
+
+    def peer(self, axis, shift):
+        at = list(self.at)
+        at[axis] = self.digit(axis, shift)
+        return (at[0] * self.digits[1] + at[1], at[2] * self.digits[3] + at[3])
+
+    def greet(self):
+        barrier = pltpu.get_barrier_semaphore()
+        peers = []
+        for axis, n in enumerate(self.digits):
+            if n > 1:
+                peers.append(self.peer(axis, 1))
+            if n > 2:
+                peers.append(self.peer(axis, -1))
+        for peer in peers:
+            pl.semaphore_signal(barrier, inc=1, device_id=peer, device_id_type=MESH)
+        pl.semaphore_wait(barrier, len(peers))
+
+
+class Sems:
+    def __init__(self, send, recv, local):
+        self.send, self.recv, self.local = send, recv, local
+        self.remotes = self.locals = 0
+
+    def remote(self, src, dst, peer):
+        copy = pltpu.make_async_remote_copy(
+            src_ref=src,
+            dst_ref=dst,
+            send_sem=self.send.at[self.remotes],
+            recv_sem=self.recv.at[self.remotes],
+            device_id=peer,
+            device_id_type=MESH,
+        )
+        self.remotes += 1
+        copy.start()
+        return copy
+
+    def copy(self, src, dst):
+        copy = pltpu.make_async_copy(src, dst, self.local.at[self.locals])
+        self.locals += 1
+        copy.start()
+        return copy
+
+
+def hops(n):
+    if n == 1:
+        return []
+    if n == 2:
+        return [(0, (1,), False)]
+    return [(s, (1, -1), s == n // 2 - 1) for s in range(n // 2)]
+
+
+def column_part(start, size, direction, halved):
+    if not halved:
+        return start, size
+    first = size // 256 * 128
+    if first == 0:
+        return (start, size) if direction > 0 else (start, 0)
+    return (start, first) if direction > 0 else (start + first, size - first)
+
+
+def slots(place, view, axis, slot, part):
+    index = []
+    for other, n in enumerate(place.digits):
+        if other == axis:
+            index.append(slot)
+        elif other in view:
+            index.append(pl.ds(0, n))
+        else:
+            index.append(place.at[other])
+    return tuple(index) + (slice(None), pl.ds(*part))
+
+
+def gather_piece(place, sems, shard, full, start, size, order):
+    held, sends, cores = set(), [], []
+    own = sems.copy(
+        shard.at[:, pl.ds(start, size)], full.at[slots(place, (), None, None, (start, size))]
+    )
+    core = place.peer(3, 1)
+
+    def forward(axis, slot, part):
+        view = full.at[slots(place, held, axis, slot, part)]
+        cores.append(sems.remote(view, view, core))
+
+    first = True
+    for axis in order:
+        n = place.digits[axis]
+        for step, directions, last in hops(n):
+            started = []
+            for direction in directions:
+                part = column_part(start, size, direction, last)
+                if part[1] == 0:
+                    continue
+                index = slots(place, held, axis, place.digit(axis, -step * direction), part)
+                src = shard.at[:, pl.ds(*part)] if first and step == 0 else full.at[index]
+                started.append(
+                    (direction, sems.remote(src, full.at[index], place.peer(axis, direction)))
+                )
+            yield
+            for direction, copy in started:
+                copy.wait_recv()
+                sends.append(copy)
+                if not first and not last and n > 2:
+                    forward(axis, place.digit(axis, -(step + 1) * direction), (start, size))
+            if not first and (last or n == 2):
+                forward(axis, place.digit(axis, n // 2), (start, size))
+        if n > 1:
+            held.add(axis)
+            if first:
+                own.wait()
+                forward(None, None, (start, size))
+                first = False
+    if first:
+        own.wait()
+        forward(None, None, (start, size))
+    yield
+    for copy in cores:
+        copy.wait()
+    for copy in sends:
+        copy.wait_send()
+
+
+def accumulate(target, source, result=None):
+    lead, dims = target.shape[:-2], target.shape
+    count = 1
+    for n in lead:
+        count *= n
+
+    def index_of(flat):
+        index = []
+        for n in reversed(lead):
+            index.append(flat % n)
+            flat = flat // n
+        return tuple(reversed(index)) + (slice(None), slice(None))
+
+    def body(flat, carry):
+        index = index_of(flat)
+        total = target[index].astype(jnp.float32) + source[index].astype(jnp.float32)
+        target[index] = total.astype(target.dtype)
+        return carry
+
+    if lead:
+        lax.fori_loop(0, count, body, 0)
+    else:
+        body(0, 0)
+
+
+def reduce_steps(digits, start, size, order):
+    left, plan = [0, 1, 2], []
+    for axis in order:
+        n = digits[axis]
+        left.remove(axis)
+        lead = tuple(digits[a] for a in left)
+        for step, directions, last in reversed(hops(n)):
+            batch = []
+            for direction in directions:
+                part = column_part(start, size, direction, last)
+                if part[1] > 0:
+                    batch.append((axis, direction, step, part, lead))
+            plan.append((tuple(left), batch))
+    return plan
+
+
+def reduce_piece(place, sems, grad, acc, landed, slabs, out, start, size, order):
+    sends = []
+    lead = (slice(None),) * 3
+    whole = (slice(None), pl.ds(start, size))
+    mine = acc.at[lead + whole]
+    other = landed.at[lead + whole]
+    own = sems.copy(grad.at[lead + (place.at[3],) + whole], mine)
+    sent = sems.remote(grad.at[lead + (place.digit(3, 1),) + whole], other, place.peer(3, 1))
+    yield
+    own.wait()
+    sent.wait_recv()
+    sends.append(sent)
+    accumulate(mine, other)
+    slabs = iter(slabs)
+    for left, batch in reduce_steps(place.digits, start, size, order):
+        started = []
+        for axis, direction, step, part, _ in batch:
+            slot = place.digit(axis, (step + 1) * direction)
+            src = acc.at[slots(place, left, axis, slot, part)[:3] + (slice(None), pl.ds(*part))]
+            dst = next(slabs)
+            sent = sems.remote(src, dst, place.peer(axis, direction))
+            started.append((axis, direction * step, part, dst, sent))
+        yield
+        for axis, shift, part, dst, sent in started:
+            sent.wait_recv()
+            sends.append(sent)
+            slot = place.digit(axis, shift)
+            view = slots(place, left, axis, slot, part)[:3] + (slice(None), pl.ds(*part))
+            accumulate(acc.at[view], dst)
+    out[:, pl.ds(start, size)] = acc[place.at[:3] + whole].astype(jnp.float32)
+    for sent in sends:
+        sent.wait_send()
+    yield
+
+
+def pieces_of(cols, wanted=4):
+    tiles = cols // 128
+    count = wanted
+    while tiles % count:
+        count -= 1
+    size = tiles // count * 128
+    return [(k * size, size) for k in range(count)]
+
+
+def run_all(generators):
+    live = list(generators)
+    while live:
+        still = []
+        for generator in live:
+            try:
+                next(generator)
+                still.append(generator)
+            except StopIteration:
+                pass
+        live = still
+
+
+def gather_kernel(digits, count, *refs):
+    shards, fulls = refs[:count], refs[count : 2 * count]
+    send, recv, local = refs[2 * count :]
+    place = Place(digits)
+    sems = Sems(send, recv, local)
+    place.greet()
+    run_all(
+        gather_piece(place, sems, shard, full, start, size, ORDERS[k % 4])
+        for shard, full in zip(shards, fulls)
+        for k, (start, size) in enumerate(pieces_of(shard.shape[1]))
+    )
+
+
+def gather_all(digits, shards):
+    count = len(shards)
+    copies = 16 * 4 * count * max(1, max(digits) // 4)
+    whole = [jax.ShapeDtypeStruct(digits + s.shape, s.dtype) for s in shards]
+    return pl.pallas_call(
+        functools.partial(gather_kernel, digits, count),
+        out_shape=whole,
+        in_specs=[pl.BlockSpec(memory_space=pl.ANY)] * count,
+        out_specs=[pl.BlockSpec(memory_space=pl.ANY)] * count,
+        scratch_shapes=[
+            pltpu.SemaphoreType.DMA((copies,)),
+            pltpu.SemaphoreType.DMA((copies,)),
+            pltpu.SemaphoreType.DMA((4 * count,)),
+        ],
+        compiler_params=pltpu.CompilerParams(collective_id=0, has_side_effects=True),
+        name="gather_all",
+    )(*shards)
+
+
+def reduce_plan(digits, grads):
+    plan = []
+    for g, grad in enumerate(grads):
+        for k, (start, size) in enumerate(pieces_of(grad.shape[-1])):
+            plan.append((g, start, size, ORDERS[k % 4]))
+    return plan
+
+
+def reduce_kernel(digits, plan, slab_counts, count, *refs):
+    grads, outs = refs[:count], refs[count : 2 * count]
+    accs, landed = refs[2 * count : 3 * count], refs[3 * count : 4 * count]
+    slabs = refs[4 * count : -3]
+    send, recv, local = refs[-3:]
+    place = Place(digits)
+    sems = Sems(send, recv, local)
+    place.greet()
+    generators, used = [], 0
+    for (g, start, size, order), many in zip(plan, slab_counts):
+        own = slabs[used : used + many]
+        used += many
+        generators.append(
+            reduce_piece(place, sems, grads[g], accs[g], landed[g], own, outs[g], start, size, order)
+        )
+    run_all(generators)
+
+
+def reduce_all(digits, grads):
+    count = len(grads)
+    plan = reduce_plan(digits, grads)
+    slabs, slab_counts = [], []
+    for g, start, size, order in plan:
+        shapes = [
+            pltpu.VMEM(lead + (grads[g].shape[-2], part[1]), grads[g].dtype)
+            for _, batch in reduce_steps(digits, start, size, order)
+            for _, _, _, part, lead in batch
+        ]
+        slabs += shapes
+        slab_counts.append(len(shapes))
+    blocks = [pltpu.VMEM(digits[:3] + g.shape[-2:], g.dtype) for g in grads]
+    copies = len(slabs) + len(plan)
+    return pl.pallas_call(
+        functools.partial(reduce_kernel, digits, plan, slab_counts, count),
+        out_shape=[jax.ShapeDtypeStruct(g.shape[-2:], jnp.float32) for g in grads],
+        in_specs=[pl.BlockSpec(memory_space=pl.ANY)] * count,
+        out_specs=[pl.BlockSpec(memory_space=pltpu.VMEM)] * count,
+        scratch_shapes=blocks
+        + blocks
+        + slabs
+        + [
+            pltpu.SemaphoreType.DMA((copies,)),
+            pltpu.SemaphoreType.DMA((copies,)),
+            pltpu.SemaphoreType.DMA((len(plan),)),
+        ],
+        compiler_params=pltpu.CompilerParams(
+            collective_id=1, has_side_effects=True, vmem_limit_bytes=58 << 20
+        ),
+        name="reduce_all",
+    )(*grads)
+
+
+def tiled_rows(rows, cols):
+    return (rows, cols) if rows % 16 == 0 else (16, rows * cols // 16)
 
 
 def layer_norm(values):
@@ -120,6 +457,7 @@
 
 
 def shards(
+    digits,
     tokens,
     lengths,
     cotangent,
@@ -133,16 +471,21 @@
     ff_bias,
     head_scale,
 ):
-    full_qkv, full_out, full_fc1, full_fc2, gain_copy, bias_copy, mid_copy, ff_copy = (
-        lax.all_gather(to_bf16(w_qkv), ("dp", "fsdp"), axis=0, tiled=True),
-        lax.all_gather(to_bf16(w_out), ("dp", "fsdp"), axis=0, tiled=True),
-        lax.all_gather(to_bf16(w_fc1), ("dp", "fsdp"), axis=0, tiled=True),
-        lax.all_gather(to_bf16(w_fc2), ("dp", "fsdp"), axis=0, tiled=True),
-        lax.all_gather(to_bf16(norm_gain), ("dp", "fsdp"), axis=1, tiled=True),
-        lax.all_gather(to_bf16(norm_bias), ("dp", "fsdp"), axis=1, tiled=True),
-        lax.all_gather(to_bf16(mid_gain), ("dp", "fsdp"), axis=0, tiled=True),
-        lax.all_gather(to_bf16(ff_bias), ("dp", "fsdp"), axis=1, tiled=True),
-    )
+    weights = (w_qkv, w_out, w_fc1, w_fc2)
+    small = jnp.concatenate([v.reshape(-1) for v in (norm_gain, norm_bias, mid_gain, ff_bias)])
+    small = jnp.pad(to_bf16(small), (0, 2048 - small.shape[0])).reshape(16, 128)
+    shards_in = [to_bf16(w).reshape(tiled_rows(*w.shape)) for w in weights] + [small]
+    gathered = gather_all(digits, shards_in)
+    full_qkv, full_out, full_fc1, full_fc2 = (
+        g.reshape((-1, w.shape[1])) for g, w in zip(gathered, weights)
+    )
+    smalls = gathered[4].reshape(-1, 2048)
+    parts, used = [], 0
+    for v in (norm_gain, norm_bias, mid_gain, ff_bias):
+        block = smalls[:, used : used + v.size].reshape((-1,) + (v.shape if v.ndim == 2 else (1,) + v.shape))
+        parts.append(block.transpose(1, 0, 2).reshape(block.shape[1], -1))
+        used += v.size
+    gain_copy, bias_copy, mid_copy, ff_copy = parts[0], parts[1], parts[2][0], parts[3]
     gains = gain_copy.astype(jnp.float32)
     biases = bias_copy.astype(jnp.float32)
     mid_gains = mid_copy.astype(jnp.float32)
@@ -185,16 +528,10 @@
     positions = jnp.arange(padded, dtype=jnp.int32)
     valid = (positions[None, :] < lengths[:, None]).astype(jnp.float32).reshape(row_total, 1)
     grad_result = cotangent.astype(jnp.float32) * valid
-    back_qkv, back_out, back_fc1, back_fc2 = (
-        lax.all_gather(to_bf16(w_qkv), ("dp", "fsdp"), axis=0, tiled=True),
-        lax.all_gather(to_bf16(w_out), ("dp", "fsdp"), axis=0, tiled=True),
-        lax.all_gather(to_bf16(w_fc1), ("dp", "fsdp"), axis=0, tiled=True),
-        lax.all_gather(to_bf16(w_fc2), ("dp", "fsdp"), axis=0, tiled=True),
-    )
     grad_branch = to_bf16(grad_result)
     grad_fc2 = row_contract(normed_mid, grad_branch)
     grad_bias_fc2 = jnp.sum(grad_branch.astype(jnp.float32), axis=0)
-    grad_mid = col_contract(grad_branch, back_fc2)
+    grad_mid = col_contract(grad_branch, full_fc2)
     _, mid_pull = jax.vjp(norm_affine, activated, mid_gains, ff_biases[1])
     grad_activated, grad_mid_gain, grad_mid_bias = mid_pull(grad_mid)
     _, gelu_pull = jax.vjp(gelu_exact, pre_act)
@@ -202,7 +539,7 @@
     grad_fc1 = row_contract(normed_ff, grad_pre)
     grad_bias_fc1 = jnp.sum(grad_pre.astype(jnp.float32), axis=0)
     grad_ff_biases = jnp.stack((grad_bias_fc1, grad_mid_bias))
-    grad_normed_ff = col_contract(grad_pre, back_fc1)
+    grad_normed_ff = col_contract(grad_pre, full_fc1)
     _, ff_pull = jax.vjp(norm_affine, residual, gains[2], biases[5])
     grad_res_part, grad_gain_ff, grad_bias_ff = ff_pull(grad_normed_ff)
     grad_residual = grad_result + grad_res_part
@@ -211,7 +548,7 @@
     grad_projection = to_bf16(grad_projection)
     grad_out_w = row_contract(mixed, grad_projection)
     grad_bias_out = jnp.sum(grad_projection.astype(jnp.float32), axis=0)
-    grad_mixed = col_contract(grad_projection, back_out).reshape(row_total, heads, head_dim)
+    grad_mixed = col_contract(grad_projection, full_out).reshape(row_total, heads, head_dim)
     grad_scale_local = jnp.sum(grad_mixed * attended, axis=(0, 2))
     grad_attended = to_bf16(grad_mixed * head_scale[None, :, None])
 
@@ -244,7 +581,7 @@
     grad_qkv = row_contract(normed_in, grad_projected)
     grad_bias_q = jnp.sum(grad_projected[:, :width].astype(jnp.float32), axis=0)
     grad_bias_v = jnp.sum(grad_projected[:, 2 * width :].astype(jnp.float32), axis=0)
-    grad_normed_in = col_contract(grad_projected, back_qkv)
+    grad_normed_in = col_contract(grad_projected, full_qkv)
     _, in_pull = jax.vjp(norm_affine, x_in, gains[0], biases[0])
     grad_x_part, grad_gain_in, grad_bias_in = in_pull(grad_normed_in)
     grad_tokens = (grad_residual + grad_x_part).astype(jnp.bfloat16)
@@ -260,17 +597,24 @@
             grad_bias_fc2,
         )
     )
-    summed = (
-        lax.psum_scatter(grad_qkv, ("dp", "fsdp"), scatter_dimension=0, tiled=True),
-        lax.psum_scatter(grad_out_w, ("dp", "fsdp"), scatter_dimension=0, tiled=True),
-        lax.psum_scatter(grad_fc1, ("dp", "fsdp"), scatter_dimension=0, tiled=True),
-        lax.psum_scatter(grad_fc2, ("dp", "fsdp"), scatter_dimension=0, tiled=True),
-        lax.psum_scatter(grad_gains, ("dp", "fsdp"), scatter_dimension=1, tiled=True),
-        lax.psum_scatter(grad_biases, ("dp", "fsdp"), scatter_dimension=1, tiled=True),
-        lax.psum_scatter(grad_mid_gain, ("dp", "fsdp"), scatter_dimension=0, tiled=True),
-        lax.psum_scatter(grad_ff_biases, ("dp", "fsdp"), scatter_dimension=1, tiled=True),
-    )
-    grad_scale = lax.psum(grad_scale_local, ("dp", "fsdp"))
+    total = digits[0] * digits[1] * digits[2] * digits[3]
+    block = []
+    for v in (grad_gains, grad_biases, grad_mid_gain[None], grad_ff_biases):
+        block.append(v.reshape(v.shape[0], total, -1).transpose(1, 0, 2).reshape(total, -1))
+    block.append(jnp.broadcast_to(grad_scale_local[None], (total, heads)))
+    block = jnp.concatenate(block, axis=1)
+    block = jnp.pad(block, ((0, 0), (0, 1024 - block.shape[1]))).reshape(digits + (8, 128))
+    grads = [
+        to_bf16(g).reshape(digits + tiled_rows(*w.shape))
+        for g, w in zip((grad_qkv, grad_out_w, grad_fc1, grad_fc2), weights)
+    ]
+    summed = reduce_all(digits, grads + [block])
+    flat, used, owned = summed[4].reshape(-1), 0, []
+    for v in (norm_gain, norm_bias, mid_gain, ff_bias, head_scale):
+        owned.append(flat[used : used + v.size].reshape(v.shape))
+        used += v.size
+    summed = [g.reshape(w.shape) for g, w in zip(summed[:4], weights)] + owned
+    grad_scale = summed[8]
     return (
         result.astype(jnp.bfloat16),
         grad_tokens,
@@ -302,7 +646,7 @@
         P(),
     )
     return jax.shard_map(
-        shards,
+        functools.partial(shards, digits_of(mesh)),
         mesh=mesh,
         in_specs=placed,
         out_specs=(

time: 1940 us -> 985 us (0.51)
  waiting for transfers between devices: 936 us -> 0 us
  Pallas kernels: 0 us -> 284 us
  blocking collectives: 192 us -> 0 us
  local copies, waits for them, and re-layouts: 189 us -> 111 us
    reduce_scatter x4 -> x0, waiting for transfers between devices: 670 us -> none  [the longest x1 187 us: shards(): lax.psum_scatter(grad_fc2, ('dp', 'fsdp'), scatter_dimension=0, tiled=True)]
    pallas_call x0 -> x2, Pallas kernels: none -> 284 us  [the longest x1 142 us: reduce_all(): pl.pallas_call(functools.partial(reduce_kernel, digits, plan, slab_counts...]
    unnamed x14 -> x0, waiting for transfers between devices: 266 us -> none
    all_gather x4 -> x0, blocking collectives: 155 us -> none  [the longest x1 43 us: shards(): lax.all_gather(to_bf16(ff_bias), ('dp', 'fsdp'), axis=1, tiled=True)]
    dynamic_update_slice x4 -> x0, local copies, waits for them, and re-layouts: 80.5 us -> none  [attend_sequence(): attended, log_totals = lax.map(one_block, (query_blocks, offsets))]
    unnamed x1 -> x0, blocking collectives: 37.3 us -> none
    unnamed x172 -> x171, local copies, waits for them, and re-layouts: 48.8 us -> 44 us
    convert_element_type x9 -> x8, other arithmetic: 70.3 us -> 68.5 us  [to_bf16(): return values.astype(jnp.bfloat16)]
  transfers between devices with their start and end apart: 11 -> 0, of which waited for: 7 -> 0; matrix products, arithmetic and copies ran while one was open for 20% -> 0% of each run, Pallas kernels for 0% -> 0%
where the time goes in v1:
time: 985 us; the launch traced here: 975 us
  matrix products  389 us (39%)
  Pallas kernels  284 us (29%)
  other arithmetic  187 us (19%)
  local copies, waits for them, and re-layouts  111 us (11%)
    pallas_call x1, Pallas kernels, reduce_all(): pl.pallas_call(functools.partial(reduce_kernel, digits, plan, slab_counts...  142 us
    pallas_call x1, Pallas kernels, gather_all(): pl.pallas_call(functools.partial(gather_kernel, digits, count), out_shape...  142 us
    dot_general x4, matrix products, plain_product(): return jnp.dot(left, right, preferred_element_type=jnp.float32)  74.6 us
    convert_element_type x8, other arithmetic, to_bf16(): return values.astype(jnp.bfloat16)  68.5 us
    dot_general x4, matrix products, score_block(): jnp.einsum('qhd,khd->hqk', query_block, key_rows, preferred_element_type=...  66.2 us
    dot_general x2, matrix products, attend_block_back(): jnp.einsum('qhd,khd->hqk', grad_block, value_rows, preferred_element_type...  51.9 us
    dot_general x4, matrix products, col_contract(): lax.dot_general(left, right, (((1,), (1,)), ((), ())), preferred_element_...  49 us
    dot_general x4, matrix products, row_contract(): lax.dot_general(left, right, (((0,), (0,)), ((), ())), preferred_element_...  46.7 us

profile of v1, /device:TPU:0, one launch (start us, length us, event | category | flops | bytes accessed | tf_op | source)
XLA Modules:
  0.0 974.6 jit_solution(6029960920537889153)
XLA Ops:
  13.6 2.9 copy.41
  17.5 4.0 copy.48
  23.1 142.1 %gather_all.1 = (bf16[4,2,2,2,32,3072]{5,4,3,2,1,0:T(8,128)(2,1)}, bf16[4,2,2,2,32,1024]{5,4,3,2,1,0:T(8,128)(2,1)}, bf16[4,2,2,2,32,4096]{5,4,3,2,1,0:T(8,128)(...) custom-call(bf16[32,3072]{1,0:T(8,128)(2,1)} %convert_element_type.152.refs_0_, ...), custom_call_target="tpu_custom_call" | custom-call | tf_op jit(solution)/shard_map/gather_all/pallas_call | solution.py:268
  172.6 9.3 fusion.82
  182.3 3.3 fusion.51
  185.6 3.9 copy.44
  189.5 3.0 copy.43
  192.5 6.4 reshape.504
  198.9 5.4 copy.45
  204.4 100.0 %while.49 = (s32[]{:T(128)}, f32[2,512,16,64]{1,3,2,0:T(8,128)}, f32[2,16,512]{2,1,0:T(8,128)S(1)}, s32[2]{0:T(128)S(1)}, s32[]{:T(128)}, /*index=5*/bf16[2,512,...) while((s32[]{:T(128)}, f32[2,512,16,64]{1,3,2,0:T(8,128)}, ...), condition=%wide.region_5.6_spmd.clone, body=%wide.region_2.5_spmd.sunk.clone | while | flops 2249188864 | bytes 143923376 | solution.py:411
  206.7 15.6 %fusion.150 = (f32[16,512]{1,0:T(8,128)S(1)}, f32[16,512,1024]{2,1,0:T(8,128)}) fusion(pred[512,1024]{1,0:T(8,128)(4,1)S(1)} %fusion.149, bf16[1024,16,64]{0,2,1:T(8,128)(2,1)} %get-tuple-element.577, bf16[2,512,16,64]{1,3,2,0:T(8,128)(2,1)} %get-tuple-element.576, s32[]{:T(128)S(6)} %copy.86), kind=kOutput, calls=%fused_computation.3.clone.1.clone | convolution fusion | flops 1098899456 | bytes 37257220 | tf_op jit(solution)/shard_map/while/body/eval_jaxpr/while/body/eval_jaxpr/qhd,khd->hqk/dot_general | solution.py:386
  222.3 15.3 %fusion.151 = f32[16,512]{1,0:T(8,128)S(1)} fusion(f32[16,512,1024]{2,1,0:T(8,128)} %get-tuple-element.517, f32[16,512]{1,0:T(8,128)S(1)} %get-tuple-element.518, pred[512,1024]{1,0:T(8,128)(4,1)S(1)} %fusion.149), kind=kLoop, calls=%fused_computation.4.clone.1.clone | loop fusion | flops 33546240 | bytes 34144256 | tf_op jit(solution)/shard_map/while/body/eval_jaxpr/while/body/eval_jaxpr/reduce_sum | solution.py:395
  237.6 14.7 %bitcast_dynamic-update-slice_fusion.9 = f32[2,512,16,64]{1,3,2,0:T(8,128)S(1)} fusion(f32[2,512,16,64]{1,3,2,0:T(8,128)S(1)} %copy-done.13, s32[]{:T(128)S(6)} %copy.86, bf16[1024,16,64]{0,2,1:T(8,128)(2,1)} %get-tuple-element.578, f32[16,512,1024]{2,1,0:T(8,128)} %get-tuple-element.517, f32[16,512]{1,0:T(8,128)S(1)} %fusion.151, ...), kind=kOutput, calls=%fused_computation.6.clone.1.clone | convolution fusion | flops 1115684864 | bytes 38338564 | tf_op jit(solution)/shard_map/while/body/eval_jaxpr/while/body/eval_jaxpr/hqk,khd->qhd/dot_general | solution.py:397
  252.3 2.0 copy-done.14
  256.6 15.6 %fusion.150 = (f32[16,512]{1,0:T(8,128)S(1)}, f32[16,512,1024]{2,1,0:T(8,128)}) fusion(pred[512,1024]{1,0:T(8,128)(4,1)S(1)} %fusion.149, bf16[1024,16,64]{0,2,1:T(8,128)(2,1)} %get-tuple-element.577, bf16[2,512,16,64]{1,3,2,0:T(8,128)(2,1)} %get-tuple-element.576, s32[]{:T(128)S(6)} %copy.86), kind=kOutput, calls=%fused_computation.3.clone.1.clone | convolution fusion | flops 1098899456 | bytes 37257220 | tf_op jit(solution)/shard_map/while/body/eval_jaxpr/while/body/eval_jaxpr/qhd,khd->hqk/dot_general | solution.py:386
  272.2 15.3 %fusion.151 = f32[16,512]{1,0:T(8,128)S(1)} fusion(f32[16,512,1024]{2,1,0:T(8,128)} %get-tuple-element.517, f32[16,512]{1,0:T(8,128)S(1)} %get-tuple-element.518, pred[512,1024]{1,0:T(8,128)(4,1)S(1)} %fusion.149), kind=kLoop, calls=%fused_computation.4.clone.1.clone | loop fusion | flops 33546240 | bytes 34144256 | tf_op jit(solution)/shard_map/while/body/eval_jaxpr/while/body/eval_jaxpr/reduce_sum | solution.py:395
  287.5 14.7 %bitcast_dynamic-update-slice_fusion.9 = f32[2,512,16,64]{1,3,2,0:T(8,128)S(1)} fusion(f32[2,512,16,64]{1,3,2,0:T(8,128)S(1)} %copy-done.13, s32[]{:T(128)S(6)} %copy.86, bf16[1024,16,64]{0,2,1:T(8,128)(2,1)} %get-tuple-element.578, f32[16,512,1024]{2,1,0:T(8,128)} %get-tuple-element.517, f32[16,512]{1,0:T(8,128)S(1)} %fusion.151, ...), kind=kOutput, calls=%fused_computation.6.clone.1.clone | convolution fusion | flops 1115684864 | bytes 38338564 | tf_op jit(solution)/shard_map/while/body/eval_jaxpr/while/body/eval_jaxpr/hqk,khd->qhd/dot_general | solution.py:397
  302.2 2.0 copy-done.14
  304.4 2.9 multiply_convert_fusion.3
  307.3 2.2 copy.46
  310.1 2.5 add_reduce_fusion
  313.4 3.0 copy-done.15
  316.4 2.5 copy.67
  318.8 3.2 copy.55
  322.1 3.1 copy.71
  330.8 48.0 %fusion.86 = (f32[1024]{0:T(1024)S(1)}, f32[1024,4096]{1,0:T(8,128)}, f32[1024,4096]{1,0:T(8,128)}, f32[1024,4096]{1,0:T(8,128)}) fusion(f32[4096]{0:T(1024)S(1)} %bitcast.229, bf16[1024,4096]{1,0:T(8,128)(2,1)S(1)} %bitcast.240, bf16[1024,1024]{0,1:T(8,128)(2,1)S(1)} %add_convert_fusion.7.clone.4), kind=kOutput, calls=%fused_computation.190 | convolution fusion | flops 8866757632 | bytes 60837888 | tf_op jit(solution)/shard_map/dot_general | solution.py:367
  378.8 21.8 %multiply_reduce_fusion.2 = (f32[1024]{0:T(1024)S(1)}, f32[1024]{0:T(1024)S(1)}, f32[4096]{0:T(1024)S(1)}, f32[1024,4096]{1,0:T(8,128)}) fusion(f32[1024,4096]{1,0:T(8,128)} %get-tuple-element.355, f32[4096]{0:T(1024)S(1)} %copy-done.28, f32[1024]{0:T(1024)S(1)} %broadcast_multiply_fusion, bf16[4096,1024]{1,0:T(8,128)(2,1)} %bitcast.241, ...), kind=kOutput, calls=%fused_computation.54 | convolution fusion | flops 8622434304 | bytes 44089344 | tf_op jit(solution)/shard_map/dot_general | solution.py:377
  400.6 13.9 %multiply_reduce_fusion.1 = (f32[4096]{0:T(1024)}, f32[1024]{0:T(1024)S(1)}) fusion(f32[1024,4096]{1,0:T(8,128)} %get-tuple-element.376, f32[1024,4096]{1,0:T(8,128)} %get-tuple-element.355, f32[1024]{0:T(1024)S(1)} %get-tuple-element.372, f32[1024]{0:T(1024)S(1)} %broadcast_multiply_fusion, f32[1024]{0:T(1024)S(1)} %get-tuple-element.371, ...), kind=kLoop, calls=%fused_computation.52 | loop fusion | flops 41937920 | bytes 33603584 | tf_op jit(solution)/shard_map/transpose(jvp())/reduce_sum | solution.py:355
  414.4 30.6 %convert_reduce_fusion = (f32[4096]{0:T(1024)S(1)}, bf16[1024,4096]{1,0:T(8,128)(2,1)}, bf16[1024,4096]{1,0:T(8,128)(2,1)}) fusion(f32[1024,4096]{1,0:T(8,128)} %get-tuple-element.356, f32[1024]{0:T(1024)S(1)} %negate_multiply_fusion.4, f32[1024]{0:T(1024)S(1)} %get-tuple-element.371, f32[1024,4096]{1,0:T(8,128)} %get-tuple-element.355, ...), kind=kLoop, calls=%fused_computation.51 | loop fusion | flops 117436416 | bytes 83968000 | tf_op jit(solution)/shard_map/reduce_sum | solution.py:540
  445.0 14.8 %add_convert_fusion.4 = bf16[1024,1024]{0,1:T(8,128)(2,1)} fusion(f32[1024,1024]{0,1:T(8,128)S(1)} %copy-done.2, f32[1024]{0:T(1024)S(1)} %copy-done.70, bf16[1024,4096]{1,0:T(8,128)(2,1)} %get-tuple-element.363, bf16[4096,1024]{1,0:T(8,128)(2,1)} %bitcast.242), kind=kOutput, calls=%fused_computation.114 | convolution fusion | flops 8593080320 | bytes 23072768 | tf_op jit(solution)/shard_map/dot_general | solution.py:367
  459.9 15.3 %fusion.91 = (f32[1024]{0:T(1024)S(1)}, f32[1024,1024]{1,0:T(8,128)}) fusion(bf16[1024,4096]{1,0:T(8,128)(2,1)} %get-tuple-element.346, bf16[1024,4096]{1,0:T(8,128)(2,1)} %bitcast.237), kind=kOutput, calls=%fused_computation.194 | convolution fusion | flops 8590982144 | bytes 20975616 | tf_op jit(solution)/shard_map/dot_general | solution.py:377
  475.8 3.9 copy.59
  480.4 5.4 copy.49
  485.8 4.2 multiply_reduce_fusion.8
  491.7 2.7 multiply_reduce_fusion.5
  494.4 15.1 %convolution_convert_fusion.1 = bf16[1024,4096]{1,0:T(8,128)(2,1)} fusion(bf16[1024,4096]{1,0:T(8,128)(2,1)} %get-tuple-element.346, f32[1024,1024]{0,1:T(8,128)S(1)} %copy-done.3, f32[1024]{0:T(1024)S(1)} %copy-done.60, f32[1024]{0:T(1024)S(1)} %copy-done.31, f32[1024]{0:T(1024)S(1)} %copy-done.39, f32[1024]{0:T(1024)S(1)} %copy-done.27), kind=kOutput, calls=%fused_computation.73 | convolution fusion | flops 8599371776 | bytes 20987904 | tf_op jit(solution)/shard_map/dot_general | solution.py:371
  509.6 5.3 multiply_reduce_fusion.6
  514.9 16.2 %convolution_convert_fusion = bf16[4096,1024]{1,0:T(8,128)(2,1)} fusion(bf16[1024,4096]{1,0:T(8,128)(2,1)} %get-tuple-element.363, bf16[1024,1024]{0,1:T(8,128)(2,1)S(1)} %copy-done.16, f32[1024]{0:T(1024)S(1)} %copy-done.66), kind=kOutput, calls=%fused_computation.72 | convolution fusion | flops 8597274624 | bytes 18878464 | tf_op jit(solution)/shard_map/dot_general | solution.py:371
  535.5 3.4 multiply_reduce_fusion.4
  538.9 3.7 fusion.59
  544.2 221.3 %while.50 = (s32[]{:T(128)}, f32[1024,16,64]{0,2,1:T(8,128)}, f32[1024,16,64]{0,2,1:T(8,128)}, bf16[2,512,16,64]{1,3,2,0:T(8,128)(2,1)}, bf16[2,512,16,64]{1,3,2...) while((s32[]{:T(128)}, f32[1024,16,64]{0,2,1:T(8,128)}, ...), condition=%wide.region_20.21_spmd.clone.clone, body=%wide.region_18.20_spmd.clone.sunk.clone | while | flops 5501347328 | bytes 350460096 | solution.py:453
  546.7 17.5 %fusion.161 = f32[16,512,1024]{2,1,0:T(8,128)} fusion(bf16[1024,16,64]{0,2,1:T(8,128)(2,1)} %get-tuple-element.608, bf16[2,512,16,64]{1,3,2,0:T(8,128)(2,1)} %get-tuple-element.605, s32[]{:T(128)S(6)} %copy.96), kind=kOutput, calls=%fused_computation.33.clone.1.clone | convolution fusion | flops 1073741824 | bytes 36700164 | tf_op jit(solution)/shard_map/while/body/eval_jaxpr/while/body/eval_jaxpr/qhd,khd->hqk/dot_general | solution.py:386
  564.2 17.5 %bitcast_add_fusion.7 = f32[1024,16,64]{0,2,1:T(8,128)} fusion(f32[1024,16,64]{0,2,1:T(8,128)} %get-tuple-element.592, f32[16,512,1024]{2,1,0:T(8,128)} %fusion.161, f32[16,512]{1,0:T(8,128)S(1)} %dynamic-slice_bitcast_fusion.3, pred[512,1024]{1,0:T(8,128)(4,1)S(1)} %fusion.162, pred[]{:T(512)S(6)} %compare.33, ...), kind=kOutput, calls=%fused_computation.24.clone.1.clone | convolution fusion | flops 1109393408 | bytes 43548676 | tf_op jit(solution)/shard_map/while/body/eval_jaxpr/while/body/eval_jaxpr/hqk,qhd->khd/dot_general | solution.py:421
  581.7 26.0 %multiply_reduce_fusion.13 = (f32[16,512]{1,0:T(8,128)S(1)}, f32[16,512,1024]{2,1,0:T(8,128)}) fusion(f32[16,512,1024]{2,1,0:T(8,128)} %fusion.161, f32[16,512]{1,0:T(8,128)S(1)} %dynamic-slice_bitcast_fusion.3, pred[512,1024]{1,0:T(8,128)(4,1)S(1)} %fusion.162, bf16[1024,16,64]{0,2,1:T(8,128)(2,1)} %get-tuple-element.611, ...), kind=kOutput, calls=%fused_computation.19.clone.1.clone | convolution fusion | flops 1115676672 | bytes 70844416 | tf_op jit(solution)/shard_map/while/body/eval_jaxpr/while/body/eval_jaxpr/qhd,khd->hqk/dot_general | solution.py:418
  607.7 27.8 %multiply_convert_fusion.9 = bf16[16,512,1024]{2,1,0:T(8,128)(2,1)} fusion(f32[16,512,1024]{2,1,0:T(8,128)} %get-tuple-element.540, f32[16,512,1024]{2,1,0:T(8,128)} %fusion.161, f32[16,512]{1,0:T(8,128)S(1)} %get-tuple-element.541, f32[16,512]{1,0:T(8,128)S(1)} %dynamic-slice_bitcast_fusion.3, pred[512,1024]{1,0:T(8,128)(4,1)S(1)} %fusion.162), kind=kLoop, calls=%fused_computation.18.clone.1.clone | loop fusion | flops 50331648 | bytes 84475904 | tf_op jit(solution)/shard_map/while/body/eval_jaxpr/while/body/eval_jaxpr/convert_element_type | solution.py:363
  635.5 10.3 %bitcast_dynamic-update-slice_fusion.11 = bf16[2,512,16,64]{1,3,2,0:T(8,128)(2,1)} fusion(bf16[2,512,16,64]{1,3,2,0:T(8,128)(2,1)} %get-tuple-element.593, s32[]{:T(128)S(6)} %copy.96, bf16[16,512,1024]{2,1,0:T(8,128)(2,1)} %multiply_convert_fusion.9, bf16[1024,16,64]{0,2,1:T(8,128)(2,1)} %get-tuple-element.608), kind=kOutput, calls=%fused_computation.26.clone.1.clone | convolution fusion | flops 1074266112 | bytes 20971524 | tf_op jit(solution)/shard_map/while/body/eval_jaxpr/while/body/eval_jaxpr/hqk,khd->qhd/dot_general | solution.py:428
  647.0 6.5 bitcast_add_fusion.6
  655.8 17.5 %fusion.161 = f32[16,512,1024]{2,1,0:T(8,128)} fusion(bf16[1024,16,64]{0,2,1:T(8,128)(2,1)} %get-tuple-element.608, bf16[2,512,16,64]{1,3,2,0:T(8,128)(2,1)} %get-tuple-element.605, s32[]{:T(128)S(6)} %copy.96), kind=kOutput, calls=%fused_computation.33.clone.1.clone | convolution fusion | flops 1073741824 | bytes 36700164 | tf_op jit(solution)/shard_map/while/body/eval_jaxpr/while/body/eval_jaxpr/qhd,khd->hqk/dot_general | solution.py:386
  673.3 18.7 %bitcast_add_fusion.7 = f32[1024,16,64]{0,2,1:T(8,128)} fusion(f32[1024,16,64]{0,2,1:T(8,128)} %get-tuple-element.592, f32[16,512,1024]{2,1,0:T(8,128)} %fusion.161, f32[16,512]{1,0:T(8,128)S(1)} %dynamic-slice_bitcast_fusion.3, pred[512,1024]{1,0:T(8,128)(4,1)S(1)} %fusion.162, pred[]{:T(512)S(6)} %compare.33, ...), kind=kOutput, calls=%fused_computation.24.clone.1.clone | convolution fusion | flops 1109393408 | bytes 43548676 | tf_op jit(solution)/shard_map/while/body/eval_jaxpr/while/body/eval_jaxpr/hqk,qhd->khd/dot_general | solution.py:421
  692.1 26.0 %multiply_reduce_fusion.13 = (f32[16,512]{1,0:T(8,128)S(1)}, f32[16,512,1024]{2,1,0:T(8,128)}) fusion(f32[16,512,1024]{2,1,0:T(8,128)} %fusion.161, f32[16,512]{1,0:T(8,128)S(1)} %dynamic-slice_bitcast_fusion.3, pred[512,1024]{1,0:T(8,128)(4,1)S(1)} %fusion.162, bf16[1024,16,64]{0,2,1:T(8,128)(2,1)} %get-tuple-element.611, ...), kind=kOutput, calls=%fused_computation.19.clone.1.clone | convolution fusion | flops 1115676672 | bytes 70844416 | tf_op jit(solution)/shard_map/while/body/eval_jaxpr/while/body/eval_jaxpr/qhd,khd->hqk/dot_general | solution.py:418
  718.1 27.8 %multiply_convert_fusion.9 = bf16[16,512,1024]{2,1,0:T(8,128)(2,1)} fusion(f32[16,512,1024]{2,1,0:T(8,128)} %get-tuple-element.540, f32[16,512,1024]{2,1,0:T(8,128)} %fusion.161, f32[16,512]{1,0:T(8,128)S(1)} %get-tuple-element.541, f32[16,512]{1,0:T(8,128)S(1)} %dynamic-slice_bitcast_fusion.3, pred[512,1024]{1,0:T(8,128)(4,1)S(1)} %fusion.162), kind=kLoop, calls=%fused_computation.18.clone.1.clone | loop fusion | flops 50331648 | bytes 84475904 | tf_op jit(solution)/shard_map/while/body/eval_jaxpr/while/body/eval_jaxpr/convert_element_type | solution.py:363
  745.9 10.3 %bitcast_dynamic-update-slice_fusion.11 = bf16[2,512,16,64]{1,3,2,0:T(8,128)(2,1)} fusion(bf16[2,512,16,64]{1,3,2,0:T(8,128)(2,1)} %get-tuple-element.593, s32[]{:T(128)S(6)} %copy.96, bf16[16,512,1024]{2,1,0:T(8,128)(2,1)} %multiply_convert_fusion.9, bf16[1024,16,64]{0,2,1:T(8,128)(2,1)} %get-tuple-element.608), kind=kOutput, calls=%fused_computation.26.clone.1.clone | convolution fusion | flops 1074266112 | bytes 20971524 | tf_op jit(solution)/shard_map/while/body/eval_jaxpr/while/body/eval_jaxpr/hqk,khd->qhd/dot_general | solution.py:428
  757.4 7.7 bitcast_add_fusion.6
  765.5 3.8 copy.53
  772.2 2.7 convert.43
  779.8 8.6 fusion.90
  788.4 11.8 %convolution_convert_fusion.2 = bf16[1024,3072]{1,0:T(8,128)(2,1)} fusion(bf16[1024,1024]{0,1:T(8,128)(2,1)} %bitcast.215, bf16[1024,1024]{0,1:T(8,128)(2,1)} %bitcast.211, bf16[1024,1024]{0,1:T(8,128)(2,1)S(1)} %bitcast.203, bf16[1024,1024]{0,1:T(8,128)(2,1)S(1)} %copy-done.6, f32[1024]{0:T(1024)S(1)} %copy-done.68, f32[1024]{0:T(1024)S(1)} %copy-done.49, ...), kind=kOutput, calls=%fused_computation.85 | convolution fusion | flops 6470762496 | bytes 14696448 | tf_op jit(solution)/shard_map/dot_general | solution.py:371
  800.7 5.3 copy.54
  806.0 3.0 fusion.50
  809.5 2.1 fusion.48
  811.6 2.7 add_convert_fusion.2
  814.3 3.9 copy.60
  819.3 142.2 %reduce_all.1 = (f32[32,3072]{1,0:T(8,128)}, f32[32,1024]{1,0:T(8,128)}, f32[32,4096]{1,0:T(8,128)}, f32[128,1024]{1,0:T(8,128)}, f32[8,128]{1,0:T(8,128)}) custom-call(bf16[4,2,2,2,32,3072]{5,4,3,2,1,0:T(8,128)(2,1)} %bitcast.206, bf16[4,2,2,2,32,1024]{5,4,3,2,1,0:T(8,128)(2,1)} %bitcast.209, bf16[4,2,2,2,32,4096]{5,4,3,2,1,0:T(8,128)(2,1)} %bitcast.199, ...), custom_call_target="tpu_custom_call" | custom-call | tf_op jit(solution)/shard_map/reduce_all/pallas_call | solution.py:323
  972.5 1.9 copy.114
  (284 shorter events, 70.4 us)
Async XLA Ops:
  16.5 156.1 %copy-start.4 = (bf16[1024,1024]{0,1:T(8,128)(2,1)}, bf16[1024,1024]{0,1:T(8,128)(2,1)S(1)}, u32[]{:S(2)}) copy-start(bf16[1024,1024]{0,1:T(8,128)(2,1)S(1)} %copy.41) | copy-start | bytes 6291460
  16.9 155.7 %copy-start.36 = (f32[1024]{0:T(1024)}, f32[1024]{0:T(1024)S(1)}, u32[]{:S(2)}) copy-start(f32[1024]{0:T(1024)S(1)} %broadcast_multiply_fusion.3) | copy-start | bytes 12292
  17.5 149.5 %copy-start.52 = (f32[1024]{0:T(1024)}, f32[1024]{0:T(1024)S(1)}, u32[]{:S(2)}) copy-start(f32[1024]{0:T(1024)S(1)} %fusion.49) | copy-start | bytes 12292
  17.5 155.1 %copy-start.50 = (f32[1024]{0:T(1024)}, f32[1024]{0:T(1024)S(1)}, u32[]{:S(2)}) copy-start(f32[1024]{0:T(1024)S(1)} %fusion.74) | copy-start | bytes 12292
  169.7 12.2 %copy-start.48 = (f32[1024]{0:T(1024)}, f32[1024]{0:T(1024)S(1)}, u32[]{:S(2)}) copy-start(f32[1024]{0:T(1024)S(1)} %mul.343) | copy-start | bytes 12292
  171.1 10.8 %copy-start.67 = (f32[1024]{0:T(1024)}, f32[1024]{0:T(1024)S(1)}, u32[]{:S(2)}) copy-start(f32[1024]{0:T(1024)S(1)} %add.202) | copy-start | bytes 12292
  204.4 100.0 %copy-start.71 = (f32[16]{0:T(128)S(1)}, f32[16]{0:T(128)}, u32[]{:S(2)}) copy-start(f32[16]{0:T(128)} %param.27) | copy-start | bytes 196
  222.3 15.3 %copy-start.13 = (f32[2,512,16,64]{1,3,2,0:T(8,128)S(1)}, f32[2,512,16,64]{1,3,2,0:T(8,128)}, u32[]{:S(2)}) copy-start(f32[2,512,16,64]{1,3,2,0:T(8,128)} %get-tuple-element.564) | copy-start | bytes 12582916 | tf_op jit(solution)/shard_map/while/body/eval_jaxpr/while
  272.2 15.3 %copy-start.13 = (f32[2,512,16,64]{1,3,2,0:T(8,128)S(1)}, f32[2,512,16,64]{1,3,2,0:T(8,128)}, u32[]{:S(2)}) copy-start(f32[2,512,16,64]{1,3,2,0:T(8,128)} %get-tuple-element.564) | copy-start | bytes 12582916 | tf_op jit(solution)/shard_map/while/body/eval_jaxpr/while
  304.4 5.1 copy-start.24
  304.4 5.1 copy-start.77
  307.3 2.8 copy-start.32
  307.3 2.8 copy-start.75
  312.7 12.6 %copy-start.7 = (f32[1024,1024]{0,1:T(8,128)}, f32[1024,1024]{0,1:T(8,128)S(1)}, u32[]{:S(2)}) copy-start(f32[1024,1024]{0,1:T(8,128)S(1)} %get-tuple-element.374) | copy-start | bytes 12582916
  312.7 3.7 copy-start.15
  312.7 12.5 %copy-start.34 = (f32[1024]{0:T(1024)}, f32[1024]{0:T(1024)S(1)}, u32[]{:S(2)}) copy-start(f32[1024]{0:T(1024)S(1)} %broadcast_multiply_fusion.2) | copy-start | bytes 12292
  313.3 5.5 copy-start.54
  316.4 8.8 copy-start.42
  322.1 3.1 copy-start.5
  322.1 3.1 copy-start.40
  322.1 3.1 copy-start.65
  325.3 3.8 slice-start
  326.9 3.8 slice-start.1
  328.0 2.7 copy-start.45
  328.1 50.7 %copy-start.38 = (f32[1024]{0:T(1024)}, f32[1024]{0:T(1024)S(1)}, u32[]{:S(2)}) copy-start(f32[1024]{0:T(1024)S(1)} %fusion.76) | copy-start | bytes 12292
  330.8 48.0 %copy-start.16 = (bf16[1024,1024]{0,1:T(8,128)(2,1)S(1)}, bf16[1024,1024]{0,1:T(8,128)(2,1)}, u32[]{:S(2)}) copy-start(bf16[1024,1024]{0,1:T(8,128)(2,1)} %copy.48) | copy-start | bytes 6291460
  330.8 48.0 %copy-start.28 = (f32[4096]{0:T(1024)S(1)}, f32[4096]{0:T(1024)}, u32[]{:S(2)}) copy-start(f32[4096]{0:T(1024)} %fusion.64) | copy-start | bytes 49156
  330.8 48.0 %copy-start.66 = (f32[1024]{0:T(1024)S(1)}, f32[1024]{0:T(1024)}, u32[]{:S(2)}) copy-start(f32[1024]{0:T(1024)} %fusion.73) | copy-start | bytes 12292
  400.6 13.9 %copy-start.44 = (f32[1,32,128]{2,0,1:T(1,128)S(1)}, f32[1,32,128]{2,0,1:T(1,128)}, u32[]{:S(2)}) copy-start(f32[1,32,128]{2,0,1:T(1,128)} %get-tuple-element.369) | copy-start | bytes 49156
  414.4 30.6 %copy-start.2 = (f32[1024,1024]{0,1:T(8,128)S(1)}, f32[1024,1024]{0,1:T(8,128)}, u32[]{:S(2)}) copy-start(f32[1024,1024]{0,1:T(8,128)} %copy-done.1) | copy-start | bytes 12582916
  414.4 30.6 %copy-start.70 = (f32[1024]{0:T(1024)S(1)}, f32[1024]{0:T(1024)}, u32[]{:S(2)}) copy-start(f32[1024]{0:T(1024)} %add.230) | copy-start | bytes 12292
  480.4 5.4 copy-start.27
  480.4 5.4 copy-start.31
  485.8 4.3 copy-start.57
  485.8 4.6 copy-start.3
  485.8 5.9 copy-start.9
  485.8 5.9 copy-start.39
  491.7 2.7 copy-start.60
  494.4 15.2 %copy-start.8 = (f32[1024,1024]{0,1:T(8,128)S(1)}, f32[1024,1024]{0,1:T(8,128)}, u32[]{:S(2)}) copy-start(f32[1024,1024]{0,1:T(8,128)} %copy-done.7) | copy-start | bytes 12582916
  494.4 15.2 %copy-start.33 = (f32[1024]{0:T(1024)S(1)}, f32[1024]{0:T(1024)}, u32[]{:S(2)}) copy-start(f32[1024]{0:T(1024)} %add.211) | copy-start | bytes 12292
  494.4 15.2 %copy-start.35 = (f32[1024]{0:T(1024)S(1)}, f32[1024]{0:T(1024)}, u32[]{:S(2)}) copy-start(f32[1024]{0:T(1024)} %copy-done.34) | copy-start | bytes 12292
  494.4 15.2 %copy-start.41 = (f32[1024]{0:T(1024)S(1)}, f32[1024]{0:T(1024)}, u32[]{:S(2)}) copy-start(f32[1024]{0:T(1024)} %mul.351) | copy-start | bytes 12292
  494.4 15.2 %copy-start.43 = (f32[1024]{0:T(1024)S(1)}, f32[1024]{0:T(1024)}, u32[]{:S(2)}) copy-start(f32[1024]{0:T(1024)} %copy-done.42) | copy-start | bytes 12292
  514.9 16.2 %copy-start.11 = (f32[1024,1024]{0,1:T(8,128)}, f32[1024,1024]{0,1:T(8,128)S(1)}, u32[]{:S(2)}) copy-start(f32[1024,1024]{0,1:T(8,128)S(1)} %get-tuple-element.353) | copy-start | bytes 12582916
  514.9 16.2 %copy-start.55 = (f32[1024]{0:T(1024)S(1)}, f32[1024]{0:T(1024)}, u32[]{:S(2)}) copy-start(f32[1024]{0:T(1024)} %copy-done.54) | copy-start | bytes 12292
  532.6 2.9 copy-start.76
  535.5 3.4 copy-start.21
  535.5 3.4 copy-start.69
  635.5 11.5 %copy-start = (bf16[16,512,1024]{2,1,0:T(8,128)(2,1)S(1)}, bf16[16,512,1024]{2,1,0:T(8,128)(2,1)}, u32[]{:S(2)}) copy-start(bf16[16,512,1024]{2,1,0:T(8,128)(2,1)} %multiply_convert_fusion.9) | copy-start | bytes 50331652 | tf_op jit(solution)/shard_map/while/body/eval_jaxpr/while
  745.9 11.5 %copy-start = (bf16[16,512,1024]{2,1,0:T(8,128)(2,1)S(1)}, bf16[16,512,1024]{2,1,0:T(8,128)(2,1)}, u32[]{:S(2)}) copy-start(bf16[16,512,1024]{2,1,0:T(8,128)(2,1)} %multiply_convert_fusion.9) | copy-start | bytes 50331652 | tf_op jit(solution)/shard_map/while/body/eval_jaxpr/while
  769.3 2.8 copy-start.61
  772.2 3.5 copy-start.19
  772.2 6.8 copy-start.74
  774.9 4.9 copy-start.18
  779.8 8.6 copy-start.6
  779.8 8.6 copy-start.37
  779.8 8.6 copy-start.49
  779.8 8.6 copy-start.51
  779.8 8.6 copy-start.68
  788.4 12.0 %copy-start.47 = (f32[1,32,32]{2,0,1:T(1,128)S(1)}, f32[1,32,32]{2,0,1:T(1,128)}, u32[]{:S(2)}) copy-start(f32[1,32,32]{2,0,1:T(1,128)} %stack.54) | copy-start | bytes 12292
  806.0 3.1 copy-start.53
  806.0 3.5 copy-start.10
  814.3 4.2 copy-start.29
  814.3 4.2 copy-start.46
  (20 other events, 38.1 us)

commit v2 on v1

--- a/solution.py
+++ b/solution.py
@@ -344,116 +344,340 @@
     return (rows, cols) if rows % 16 == 0 else (16, rows * cols // 16)
 
 
-def layer_norm(values):
-    average = jnp.mean(values, axis=-1, keepdims=True)
-    centered = values - average
-    variance = jnp.mean(centered * centered, axis=-1, keepdims=True)
-    return centered * lax.rsqrt(variance + epsilon)
-
-
-def norm_affine(values, gain, offset):
-    return layer_norm(values) * gain + offset
-
-
-def gelu_exact(values):
-    return jax.nn.gelu(values, approximate=False)
-
-
 def to_bf16(values):
     return values.astype(jnp.bfloat16)
 
 
-def plain_product(left, right):
-    return jnp.dot(left, right, preferred_element_type=jnp.float32)
-
-
-def row_contract(left, right):
-    return lax.dot_general(
-        left, right, (((0,), (0,)), ((), ())), preferred_element_type=jnp.float32
-    )
-
-
-def col_contract(left, right):
-    return lax.dot_general(
-        left, right, (((1,), (1,)), ((), ())), preferred_element_type=jnp.float32
-    )
-
-
-def score_block(query_block, key_rows, offset, seq_len):
-    query_pos = offset + jnp.arange(query_block.shape[0], dtype=jnp.int32)
-    key_pos = jnp.arange(key_rows.shape[0], dtype=jnp.int32)
-    allowed = (key_pos[None, :] <= query_pos[:, None]) & (key_pos[None, :] < seq_len)
-    scores = jnp.einsum("qhd,khd->hqk", query_block, key_rows, preferred_element_type=jnp.float32)
-    scores = scores * query_block.shape[2] ** (-0.5)
-    return jnp.where(allowed[None], scores, mask_fill)
-
-
-def attend_block(query_block, key_rows, value_rows, offset, seq_len):
-    scores = score_block(query_block, key_rows, offset, seq_len)
-    row_max = jnp.max(scores, axis=-1, keepdims=True)
-    shifted = jnp.exp(scores - row_max)
-    row_sum = jnp.sum(shifted, axis=-1, keepdims=True)
-    weights = to_bf16(shifted / row_sum)
-    attended = jnp.einsum("hqk,khd->qhd", weights, value_rows, preferred_element_type=jnp.float32)
-    return (attended, (row_max + jnp.log(row_sum))[..., 0])
-
-
-def attend_sequence(query_rows, key_rows, value_rows, seq_len):
-    padded = query_rows.shape[0]
-    block_rows = min(512, padded)
-    blocks = padded // block_rows
-    query_blocks = query_rows.reshape((blocks, block_rows) + query_rows.shape[1:])
-    offsets = jnp.arange(blocks, dtype=jnp.int32) * block_rows
-
-    def one_block(pieces):
-        return attend_block(pieces[0], key_rows, value_rows, pieces[1], seq_len)
-
-    attended, log_totals = lax.map(one_block, (query_blocks, offsets))
-    return (attended.reshape(query_rows.shape), log_totals)
-
-
-def attend_block_back(query_block, key_rows, value_rows, grad_block, log_total, offset, seq_len):
-    scores = score_block(query_block, key_rows, offset, seq_len)
-    softmaxed = jnp.exp(scores - log_total[..., None])
-    grad_weights = jnp.einsum(
-        "qhd,khd->hqk", grad_block, value_rows, preferred_element_type=jnp.float32
-    )
-    grad_values = jnp.einsum(
-        "hqk,qhd->khd", to_bf16(softmaxed), grad_block, preferred_element_type=jnp.float32
-    )
-    centered = grad_weights - jnp.sum(softmaxed * grad_weights, axis=-1, keepdims=True)
-    grad_scores = to_bf16(softmaxed * centered)
-    scaling = query_block.shape[2] ** (-0.5)
-    grad_queries = (
-        jnp.einsum("hqk,khd->qhd", grad_scores, key_rows, preferred_element_type=jnp.float32)
-        * scaling
-    )
-    grad_keys = (
-        jnp.einsum("hqk,qhd->khd", grad_scores, query_block, preferred_element_type=jnp.float32)
-        * scaling
-    )
-    return (grad_queries, grad_keys, grad_values)
-
-
-def attend_sequence_back(query_rows, key_rows, value_rows, grad_rows, log_totals, seq_len):
-    padded = query_rows.shape[0]
-    block_rows = min(512, padded)
-    blocks = padded // block_rows
-    query_blocks = query_rows.reshape((blocks, block_rows) + query_rows.shape[1:])
-    grad_blocks = grad_rows.reshape((blocks, block_rows) + grad_rows.shape[1:])
-    offsets = jnp.arange(blocks, dtype=jnp.int32) * block_rows
-
-    def step_block(totals, pieces):
-        grad_queries, grad_keys, grad_values = attend_block_back(
-            pieces[0], key_rows, value_rows, pieces[1], pieces[2], pieces[3], seq_len
+def dot_nn(a, b):
+    return lax.dot_general(a, b, (((1,), (0,)), ((), ())), preferred_element_type=jnp.float32)
+
+
+def dot_nt(a, b):
+    return lax.dot_general(a, b, (((1,), (1,)), ((), ())), preferred_element_type=jnp.float32)
+
+
+def dot_tn(a, b):
+    return lax.dot_general(a, b, (((0,), (0,)), ((), ())), preferred_element_type=jnp.float32)
+
+
+def row_mean(v):
+    return jnp.mean(v, axis=-1, keepdims=True)
+
+
+def norm_parts(v):
+    centered = v - row_mean(v)
+    inverse = lax.rsqrt(row_mean(centered * centered) + epsilon)
+    return centered * inverse, inverse
+
+
+def norm_back(grad, gain, normed, inverse):
+    scaled = grad * gain
+    return (scaled - row_mean(scaled) - normed * row_mean(scaled * normed)) * inverse
+
+
+def fold(v):
+    return v.reshape(v.shape[0] // 8, 8, v.shape[1]).sum(0)
+
+
+def ffn_kernel(
+    chunk, unrolled,
+    len_ref, scale_ref, x_ref, z_ref, cot_ref, wo_ref, w1_ref, w2_ref, gain_ref, bias_ref, mid_ref, ffb_ref,
+    out_ref, c_ref, m_ref, df_ref, dy_ref, dr_ref, do_ref, sums_ref, wide_ref,
+    act_ref, slope_ref, dm_ref,
+):
+    step = pl.program_id(0)
+    rows, width = x_ref.shape
+    hidden = w1_ref.shape[1]
+    f32, bf16 = jnp.float32, jnp.bfloat16
+
+    @pl.when(step == 0)
+    def _():
+        sums_ref[...] = jnp.zeros_like(sums_ref)
+        wide_ref[...] = jnp.zeros_like(wide_ref)
+
+    def each(body, carry):
+        if unrolled:
+            for j in range(hidden // chunk):
+                carry = body(slice(j * chunk, (j + 1) * chunk), carry)
+            return carry
+        return lax.fori_loop(
+            0, hidden // chunk, lambda j, c: body(pl.ds(pl.multiple_of(j * chunk, chunk), chunk), c), carry
         )
-        return ((totals[0] + grad_keys, totals[1] + grad_values), grad_queries)
-
-    zeros_kv = jnp.zeros(key_rows.shape, jnp.float32)
-    (grad_keys, grad_values), grad_queries = lax.scan(
-        step_block, (zeros_kv, zeros_kv), (query_blocks, grad_blocks, log_totals, offsets)
-    )
-    return (grad_queries.reshape(query_rows.shape), grad_keys, grad_values)
+
+    gain = lambda k: gain_ref[k : k + 1, :]
+    bias = lambda k: bias_ref[k : k + 1, :]
+    y_norm, y_inv = norm_parts(dot_nn(z_ref[...], wo_ref[...]) + bias(3))
+    residual = x_ref[...].astype(f32) + (y_norm * gain(1) + bias(4))
+    r_norm, r_inv = norm_parts(residual)
+    normed = (r_norm * gain(2) + bias(5)).astype(bf16)
+    c_ref[...] = normed
+
+    def expand(at, total):
+        pre = dot_nn(normed, w1_ref[:, at]) + ffb_ref[0:1, at]
+        cdf = 0.5 * (1.0 + lax.erf(pre * (0.5**0.5)))
+        pdf = jnp.exp(pre * pre * -0.5) * 0.3989422804014327
+        act = pre * cdf
+        act_ref[:, at] = act
+        slope_ref[:, at] = cdf + pre * pdf
+        return total + jnp.sum(act, axis=-1, keepdims=True)
+
+    zero = jnp.zeros((rows, 1), f32)
+    average = each(expand, zero) / hidden
+
+    def spread(at, total):
+        centered = act_ref[:, at] - average
+        return total + jnp.sum(centered * centered, axis=-1, keepdims=True)
+
+    m_inv = lax.rsqrt(each(spread, zero) / hidden + epsilon)
+
+    def contract(at, total):
+        n = (act_ref[:, at] - average) * m_inv
+        act_ref[:, at] = n
+        m = (n * mid_ref[0:1, at] + ffb_ref[1:2, at]).astype(bf16)
+        m_ref[:, at] = m
+        return total + dot_nn(m, w2_ref[at, :])
+
+    branch = each(contract, jnp.zeros((rows, width), f32))
+    out_ref[...] = (residual + (branch + bias(6))).astype(bf16)
+
+    position = step * rows + lax.broadcasted_iota(jnp.int32, (rows, 1), 0)
+    d_out = jnp.where(position < len_ref[0], cot_ref[...].astype(f32), 0.0)
+    d_w = d_out.astype(bf16)
+    sums_ref[6] += fold(d_out)
+
+    def back_mid(at, totals):
+        dm = dot_nt(d_w, w2_ref[at, :])
+        n = act_ref[:, at]
+        dn = dm * n
+        wide_ref[0, :, at] += fold(dn)
+        wide_ref[2, :, at] += fold(dm)
+        g = mid_ref[0:1, at]
+        dm_ref[:, at] = dm
+        return (
+            totals[0] + jnp.sum(dm * g, axis=-1, keepdims=True),
+            totals[1] + jnp.sum(dn * g, axis=-1, keepdims=True),
+        )
+
+    first, second = each(back_mid, (zero, zero))
+    first, second = first / hidden, second / hidden
+
+    def back_act(at, total):
+        du = (dm_ref[:, at] * mid_ref[0:1, at] - first - act_ref[:, at] * second) * m_inv
+        df = (du * slope_ref[:, at]).astype(bf16)
+        df_ref[:, at] = df
+        wide_ref[1, :, at] += fold(df.astype(f32))
+        return total + dot_nt(df, w1_ref[:, at])
+
+    d_c = each(back_act, jnp.zeros((rows, width), f32))
+    sums_ref[2] += fold(d_c * r_norm)
+    sums_ref[5] += fold(d_c)
+    d_r = d_out + norm_back(d_c, gain(2), r_norm, r_inv)
+    dr_ref[...] = d_r
+    sums_ref[1] += fold(d_r * y_norm)
+    sums_ref[4] += fold(d_r)
+    d_y = norm_back(d_r, gain(1), y_norm, y_inv).astype(bf16)
+    dy_ref[...] = d_y
+    sums_ref[3] += fold(d_y.astype(f32))
+    do_ref[...] = (dot_nt(d_y, wo_ref[...]) * scale_ref[...]).astype(bf16)
+
+
+def ffn(lengths, scale_row, x, z, cot, wo, w1, w2, gains, biases, mid, ffb, rows=256, chunk=512, unrolled=True):
+    tokens, width = x.shape
+    hidden = w1.shape[1]
+    by_row = lambda n: pl.BlockSpec((rows, n), lambda i: (i, 0))
+    whole = lambda a: pl.BlockSpec(a.shape, lambda i: (0,) * a.ndim, pipeline_mode=pl.Buffered(1))
+    sds = jax.ShapeDtypeStruct
+    bf16, f32 = jnp.bfloat16, jnp.float32
+    outs = [(width, bf16), (width, bf16), (hidden, bf16), (hidden, bf16), (width, bf16), (width, f32), (width, bf16)]
+    return pl.pallas_call(
+        functools.partial(ffn_kernel, chunk, unrolled),
+        grid=(tokens // rows,),
+        in_specs=[pl.BlockSpec(memory_space=pltpu.SMEM), whole(scale_row)]
+        + [by_row(width)] * 3
+        + [whole(a) for a in (wo, w1, w2, gains, biases, mid, ffb)],
+        out_specs=[by_row(n) for n, _ in outs]
+        + [pl.BlockSpec((7, 8, width), lambda i: (0, 0, 0)), pl.BlockSpec((3, 8, hidden), lambda i: (0, 0, 0))],
+        out_shape=[sds((tokens, n), d) for n, d in outs] + [sds((7, 8, width), f32), sds((3, 8, hidden), f32)],
+        scratch_shapes=[pltpu.VMEM((rows, hidden), f32)] * 3,
+        compiler_params=pltpu.CompilerParams(vmem_limit_bytes=60 << 20),
+        name="ffn_both",
+    )(lengths, scale_row, x, z, cot, wo, w1, w2, gains, biases, mid, ffb)
+
+
+head_size = 64
+
+
+def head_lanes(values, second):
+    lane = lax.broadcasted_iota(jnp.int32, values.shape, 1)
+    keep = lane >= head_size if second else lane < head_size
+    return jnp.where(keep, values, jnp.zeros_like(values))
+
+
+def masked_scores(keys, queries, first, length):
+    scores = dot_nt(keys, queries)
+    key_pos = lax.broadcasted_iota(jnp.int32, scores.shape, 0)
+    near = key_pos[first:]
+    query_pos = first + lax.broadcasted_iota(jnp.int32, near.shape, 1)
+    last = jnp.where((near <= query_pos) & (near < length), scores[first:], mask_fill)
+    if first == 0:
+        return last
+    return jnp.concatenate((jnp.where(key_pos[:first] < length, scores[:first], mask_fill), last), axis=0)
+
+
+def attend_kernel(block, scaling, len_ref, scale_ref, q_ref, k_ref, v_ref, z_ref, log_ref):
+    length, pair = len_ref[0], pl.program_id(0)
+    tokens, lanes = q_ref.shape
+    for first in range(0, tokens, block):
+        rows, seen = slice(first, first + block), first + block
+        keys, values = k_ref[:seen, :], v_ref[:seen, :]
+        mixed = []
+        for h in range(2):
+            queries = head_lanes(q_ref[rows, :], h) * jnp.bfloat16(scaling)
+            scores = masked_scores(keys, queries, first, length)
+            top = jnp.max(scores, axis=0, keepdims=True)
+            shifted = jnp.exp(scores - top)
+            total = jnp.sum(shifted, axis=0, keepdims=True)
+            log_ref[0, h : h + 1, rows] = top + jnp.log(total)
+            attended = dot_tn(shifted.astype(jnp.bfloat16), values)
+            mixed.append(attended * (scale_ref[pair * 2 + h] / total).T)
+        lane = lax.broadcasted_iota(jnp.int32, (block, lanes), 1)
+        z_ref[rows, :] = jnp.where(lane < head_size, mixed[0], mixed[1]).astype(jnp.bfloat16)
+
+
+def attend(lengths, head_scale, qkv, block=256):
+    tokens, width = qkv.shape[0], qkv.shape[1] // 3
+    pairs = width // 128
+    cols = lambda part: pl.BlockSpec((tokens, 128), lambda p: (0, p + part * pairs))
+    smem = pl.BlockSpec(memory_space=pltpu.SMEM)
+    return pl.pallas_call(
+        functools.partial(attend_kernel, min(block, tokens), head_size**-0.5),
+        grid=(pairs,),
+        in_specs=[smem, smem, cols(0), cols(1), cols(2)],
+        out_specs=[cols(0), pl.BlockSpec((1, 2, tokens), lambda p: (p, 0, 0))],
+        out_shape=[
+            jax.ShapeDtypeStruct((tokens, width), jnp.bfloat16),
+            jax.ShapeDtypeStruct((pairs, 2, tokens), jnp.float32),
+        ],
+        compiler_params=pltpu.CompilerParams(vmem_limit_bytes=56 << 20),
+        name="attend",
+    )(lengths, head_scale, qkv, qkv, qkv)
+
+
+def attend_back_kernel(block, scaling, len_ref, q_ref, k_ref, v_ref, do_ref, log_ref, dqkv_ref, dot_ref, dk_ref, dv_ref):
+    length = len_ref[0]
+    tokens, lanes = q_ref.shape
+    bf16 = jnp.bfloat16
+    for first in range(0, tokens, block):
+        rows, seen = slice(first, first + block), first + block
+        keys, values = k_ref[:seen, :], v_ref[:seen, :]
+        mixed = []
+        for h in range(2):
+            queries = head_lanes(q_ref[rows, :], h) * bf16(scaling)
+            grads = head_lanes(do_ref[rows, :], h)
+            scores = masked_scores(keys, queries, first, length)
+            weights = jnp.exp(scores - log_ref[0, h : h + 1, rows])
+            products = weights * dot_nt(values, grads)
+            total = jnp.sum(products, axis=0, keepdims=True)
+            dot_ref[0, h : h + 1, rows] = total
+            d_scores = (products - weights * total).astype(bf16)
+            for ref, left, right in ((dv_ref, weights.astype(bf16), grads), (dk_ref, d_scores, queries)):
+                part = dot_nn(left, right)
+                if h == 0:
+                    ref[rows, :] = part[first:]
+                    if first:
+                        ref[:first, :] += part[:first]
+                else:
+                    ref[:seen, :] += part
+            mixed.append(dot_tn(d_scores, keys))
+        lane = lax.broadcasted_iota(jnp.int32, (block, lanes), 1)
+        dqkv_ref[0, rows, :] = (jnp.where(lane < head_size, mixed[0], mixed[1]) * scaling).astype(bf16)
+    dqkv_ref[1] = dk_ref[...].astype(bf16)
+    dqkv_ref[2] = dv_ref[...].astype(bf16)
+
+
+def attend_back(lengths, qkv, d_attended, logs, block=256):
+    tokens, width = qkv.shape[0], qkv.shape[1] // 3
+    pairs = width // 128
+    cols = lambda part: pl.BlockSpec((tokens, 128), lambda p: (0, p + part * pairs))
+    per_pair = pl.BlockSpec((1, 2, tokens), lambda p: (p, 0, 0))
+    return pl.pallas_call(
+        functools.partial(attend_back_kernel, min(block, tokens), head_size**-0.5),
+        grid=(pairs,),
+        in_specs=[pl.BlockSpec(memory_space=pltpu.SMEM), cols(0), cols(1), cols(2), cols(0), per_pair],
+        out_specs=[pl.BlockSpec((3, tokens, 128), lambda p: (0, 0, p)), per_pair],
+        out_shape=[
+            jax.ShapeDtypeStruct((3, tokens, width), jnp.bfloat16),
+            jax.ShapeDtypeStruct((pairs, 2, tokens), jnp.float32),
+        ],
+        scratch_shapes=[pltpu.VMEM((tokens, 128), jnp.float32)] * 2,
+        compiler_params=pltpu.CompilerParams(vmem_limit_bytes=56 << 20),
+        name="attend_back",
+    )(lengths, qkv, qkv, qkv, d_attended, logs)
+
+
+def project_kernel(x_ref, w_ref, gain_ref, bias_ref, a_ref, qkv_ref):
+    width = x_ref.shape[1]
+    normed, _ = norm_parts(x_ref[...].astype(jnp.float32))
+    a = (normed * gain_ref[0:1, :] + bias_ref[0:1, :]).astype(jnp.bfloat16)
+    a_ref[...] = a
+    for part, row in ((0, 1), (1, None), (2, 2)):
+        at = slice(part * width, (part + 1) * width)
+        value = dot_nn(a, w_ref[:, at])
+        if row is not None:
+            value = value + bias_ref[row : row + 1, :]
+        qkv_ref[:, at] = value.astype(jnp.bfloat16)
+
+
+def project(x, w, gains, biases, rows=256):
+    tokens, width = x.shape
+    by_row = lambda n: pl.BlockSpec((rows, n), lambda i: (i, 0))
+    whole = lambda a: pl.BlockSpec(a.shape, lambda i: (0,) * a.ndim, pipeline_mode=pl.Buffered(1))
+    return pl.pallas_call(
+        project_kernel,
+        grid=(tokens // rows,),
+        in_specs=[by_row(width), whole(w), whole(gains), whole(biases)],
+        out_specs=[by_row(width), by_row(3 * width)],
+        out_shape=[
+            jax.ShapeDtypeStruct((tokens, width), jnp.bfloat16),
+            jax.ShapeDtypeStruct((tokens, 3 * width), jnp.bfloat16),
+        ],
+        compiler_params=pltpu.CompilerParams(vmem_limit_bytes=56 << 20),
+        name="project",
+    )(x, w, gains, biases)
+
+
+def project_back_kernel(d_ref, x_ref, dr_ref, w_ref, gain_ref, dx_ref, sums_ref):
+    @pl.when(pl.program_id(0) == 0)
+    def _():
+        sums_ref[...] = jnp.zeros_like(sums_ref)
+
+    width = x_ref.shape[1]
+    d_a = sum(dot_nt(d_ref[k], w_ref[:, k * width : (k + 1) * width]) for k in range(3))
+    normed, inverse = norm_parts(x_ref[...].astype(jnp.float32))
+    sums_ref[0] += fold(d_a * normed)
+    sums_ref[1] += fold(d_a)
+    sums_ref[2] += fold(d_ref[0].astype(jnp.float32))
+    sums_ref[3] += fold(d_ref[2].astype(jnp.float32))
+    back = norm_back(d_a, gain_ref[0:1, :], normed, inverse)
+    dx_ref[...] = (dr_ref[...] + back).astype(jnp.bfloat16)
+
+
+def project_back(d_qkv, x, d_r, w, gains, rows=256):
+    tokens, width = x.shape
+    by_row = pl.BlockSpec((rows, width), lambda i: (i, 0))
+    whole = lambda a: pl.BlockSpec(a.shape, lambda i: (0,) * a.ndim, pipeline_mode=pl.Buffered(1))
+    return pl.pallas_call(
+        project_back_kernel,
+        grid=(tokens // rows,),
+        in_specs=[pl.BlockSpec((3, rows, width), lambda i: (0, i, 0)), by_row, by_row, whole(w), whole(gains)],
+        out_specs=[by_row, pl.BlockSpec((4, 8, width), lambda i: (0, 0, 0))],
+        out_shape=[
+            jax.ShapeDtypeStruct((tokens, width), jnp.bfloat16),
+            jax.ShapeDtypeStruct((4, 8, width), jnp.float32),
+        ],
+        compiler_params=pltpu.CompilerParams(vmem_limit_bytes=56 << 20),
+        name="project_back",
+    )(d_qkv, x, d_r, w, gains)
 
 
 def shards(
@@ -486,117 +710,29 @@
         parts.append(block.transpose(1, 0, 2).reshape(block.shape[1], -1))
         used += v.size
     gain_copy, bias_copy, mid_copy, ff_copy = parts[0], parts[1], parts[2][0], parts[3]
-    gains = gain_copy.astype(jnp.float32)
-    biases = bias_copy.astype(jnp.float32)
-    mid_gains = mid_copy.astype(jnp.float32)
-    ff_biases = ff_copy.astype(jnp.float32)
-    seq_total = lengths.shape[0]
-    row_total = tokens.shape[0]
-    padded = row_total // seq_total
-    width = tokens.shape[1]
+    f32 = jnp.float32
+    gains, biases = gain_copy.astype(f32), bias_copy.astype(f32)
+    mid_gains, ff_biases = mid_copy[None].astype(f32), ff_copy.astype(f32)
     heads = head_scale.shape[0]
-    head_dim = width // heads
-    seq_shape = (seq_total, padded, heads, head_dim)
-    x_in = tokens.astype(jnp.float32)
-    normed_in = to_bf16(norm_affine(x_in, gains[0], biases[0]))
-    projected = plain_product(normed_in, full_qkv)
-    queries = to_bf16(projected[:, :width] + biases[1])
-    key_rows = to_bf16(projected[:, width : 2 * width])
-    value_rows = to_bf16(projected[:, 2 * width :] + biases[2])
-
-    def forward_sequence(pieces):
-        return attend_sequence(pieces[0], pieces[1], pieces[2], pieces[3])
-
-    attended, log_totals = lax.map(
-        forward_sequence,
-        (
-            queries.reshape(seq_shape),
-            key_rows.reshape(seq_shape),
-            value_rows.reshape(seq_shape),
-            lengths,
-        ),
+    scale_row = jnp.repeat(head_scale, tokens.shape[1] // heads)[None]
+    normed_in, qkv = project(tokens, full_qkv, gains, biases)
+    mixed, logs = attend(lengths, head_scale, qkv)
+    result, normed_ff, normed_mid, grad_pre, grad_projection, grad_residual, grad_attended, sums, wide = ffn(
+        lengths, scale_row, tokens, mixed, cotangent, full_out, full_fc1, full_fc2, gains, biases, mid_gains, ff_biases
     )
-    attended = attended.reshape(row_total, heads, head_dim)
-    mixed = to_bf16((attended * head_scale[None, :, None]).reshape(row_total, width))
-    projection = plain_product(mixed, full_out) + biases[3]
-    residual = x_in + norm_affine(projection, gains[1], biases[4])
-    normed_ff = to_bf16(norm_affine(residual, gains[2], biases[5]))
-    pre_act = plain_product(normed_ff, full_fc1) + ff_biases[0]
-    activated = gelu_exact(pre_act)
-    normed_mid = to_bf16(norm_affine(activated, mid_gains, ff_biases[1]))
-    result = residual + (plain_product(normed_mid, full_fc2) + biases[6])
-    positions = jnp.arange(padded, dtype=jnp.int32)
-    valid = (positions[None, :] < lengths[:, None]).astype(jnp.float32).reshape(row_total, 1)
-    grad_result = cotangent.astype(jnp.float32) * valid
-    grad_branch = to_bf16(grad_result)
-    grad_fc2 = row_contract(normed_mid, grad_branch)
-    grad_bias_fc2 = jnp.sum(grad_branch.astype(jnp.float32), axis=0)
-    grad_mid = col_contract(grad_branch, full_fc2)
-    _, mid_pull = jax.vjp(norm_affine, activated, mid_gains, ff_biases[1])
-    grad_activated, grad_mid_gain, grad_mid_bias = mid_pull(grad_mid)
-    _, gelu_pull = jax.vjp(gelu_exact, pre_act)
-    grad_pre = to_bf16(gelu_pull(grad_activated)[0])
-    grad_fc1 = row_contract(normed_ff, grad_pre)
-    grad_bias_fc1 = jnp.sum(grad_pre.astype(jnp.float32), axis=0)
-    grad_ff_biases = jnp.stack((grad_bias_fc1, grad_mid_bias))
-    grad_normed_ff = col_contract(grad_pre, full_fc1)
-    _, ff_pull = jax.vjp(norm_affine, residual, gains[2], biases[5])
-    grad_res_part, grad_gain_ff, grad_bias_ff = ff_pull(grad_normed_ff)
-    grad_residual = grad_result + grad_res_part
-    _, post_pull = jax.vjp(norm_affine, projection, gains[1], biases[4])
-    grad_projection, grad_gain_post, grad_bias_post = post_pull(grad_residual)
-    grad_projection = to_bf16(grad_projection)
-    grad_out_w = row_contract(mixed, grad_projection)
-    grad_bias_out = jnp.sum(grad_projection.astype(jnp.float32), axis=0)
-    grad_mixed = col_contract(grad_projection, full_out).reshape(row_total, heads, head_dim)
-    grad_scale_local = jnp.sum(grad_mixed * attended, axis=(0, 2))
-    grad_attended = to_bf16(grad_mixed * head_scale[None, :, None])
-
-    def backward_sequence(pieces):
-        return attend_sequence_back(
-            pieces[0], pieces[1], pieces[2], pieces[3], pieces[4], pieces[5]
-        )
-
-    grad_queries, grad_keys, grad_values = lax.map(
-        backward_sequence,
-        (
-            queries.reshape(seq_shape),
-            key_rows.reshape(seq_shape),
-            value_rows.reshape(seq_shape),
-            grad_attended.reshape(seq_shape),
-            log_totals,
-            lengths,
-        ),
-    )
-    grad_projected = to_bf16(
-        jnp.concatenate(
-            (
-                grad_queries.reshape(row_total, width),
-                grad_keys.reshape(row_total, width),
-                grad_values.reshape(row_total, width),
-            ),
-            axis=1,
-        )
-    )
-    grad_qkv = row_contract(normed_in, grad_projected)
-    grad_bias_q = jnp.sum(grad_projected[:, :width].astype(jnp.float32), axis=0)
-    grad_bias_v = jnp.sum(grad_projected[:, 2 * width :].astype(jnp.float32), axis=0)
-    grad_normed_in = col_contract(grad_projected, full_qkv)
-    _, in_pull = jax.vjp(norm_affine, x_in, gains[0], biases[0])
-    grad_x_part, grad_gain_in, grad_bias_in = in_pull(grad_normed_in)
-    grad_tokens = (grad_residual + grad_x_part).astype(jnp.bfloat16)
-    grad_gains = jnp.stack((grad_gain_in, grad_gain_post, grad_gain_ff))
-    grad_biases = jnp.stack(
-        (
-            grad_bias_in,
-            grad_bias_q,
-            grad_bias_v,
-            grad_bias_out,
-            grad_bias_post,
-            grad_bias_ff,
-            grad_bias_fc2,
-        )
-    )
+    positions = jnp.arange(tokens.shape[0], dtype=jnp.int32)[:, None]
+    grad_branch = jnp.where(positions < lengths, cotangent, jnp.zeros_like(cotangent))
+    grad_fc2 = dot_tn(normed_mid, grad_branch)
+    grad_fc1 = dot_tn(normed_ff, grad_pre)
+    grad_out_w = dot_tn(mixed, grad_projection)
+    d_qkv, dots = attend_back(lengths, qkv, grad_attended, logs)
+    grad_tokens, first_sums = project_back(d_qkv, tokens, grad_residual, full_qkv, gains)
+    grad_qkv = jnp.concatenate([dot_tn(normed_in, d_qkv[k]) for k in range(3)], axis=1)
+    sums, wide, first_sums = sums.sum(1), wide.sum(1), first_sums.sum(1)
+    grad_scale_local = dots.sum(-1).reshape(heads) / head_scale
+    grad_gains = jnp.concatenate((first_sums[0:1], sums[1:3]))
+    grad_biases = jnp.concatenate((first_sums[1:4], sums[3:7]))
+    grad_mid_gain, grad_ff_biases = wide[0], wide[1:3]
     total = digits[0] * digits[1] * digits[2] * digits[3]
     block = []
     for v in (grad_gains, grad_biases, grad_mid_gain[None], grad_ff_biases):
@@ -616,7 +752,7 @@
     summed = [g.reshape(w.shape) for g, w in zip(summed[:4], weights)] + owned
     grad_scale = summed[8]
     return (
-        result.astype(jnp.bfloat16),
+        result,
         grad_tokens,
         summed[0],
         summed[1],

time: 985 us -> 535 us (0.54)
  matrix products: 389 us -> 39.3 us
  other arithmetic: 187 us -> 15.6 us
  Pallas kernels: 284 us -> 449 us
  local copies, waits for them, and re-layouts: 111 us -> 21.5 us
    dot_general x26 -> x6, matrix products: 389 us -> 39.3 us  [dot_tn(): lax.dot_general(a, b, (((0,), (0,)), ((), ())), preferred_element_type=jn...]
    pallas_call x0 -> x5, Pallas kernels: none -> 165 us  [the longest x1 70.8 us: ffn(): pl.pallas_call(functools.partial(ffn_kernel, chunk, unrolled), grid=(toke...]
    reduce_sum x19 -> x4, other arithmetic: 99.8 us -> 1.38 us  [the longest x3 1.28 us: shards(): sums, wide, first_sums = (sums.sum(1), wide.sum(1), first_sums.sum(1))]
    convert_element_type x8 -> x4, other arithmetic: 68.5 us -> 5.95 us  [to_bf16(): return values.astype(jnp.bfloat16)]
    unnamed x171 -> x46, local copies, waits for them, and re-layouts: 44 us -> 7.71 us
    while x14 -> x0, local copies, waits for them, and re-layouts: 15.2 us -> none  [the longest x2 8.69 us: attend_sequence(): attended, log_totals = lax.map(one_block, (query_blocks, offsets))]
    reshape x3 -> x1, local copies, waits for them, and re-layouts: 10.4 us -> 0.08 us  [shards(): grad_scale_local = dots.sum(-1).reshape(heads) / head_scale]
where the time goes in v2:
time: 535 us; the launch traced here: 528 us
  Pallas kernels  449 us (84%)
  matrix products  39.3 us (7%)
  local copies, waits for them, and re-layouts  21.5 us (4%)
  other arithmetic  15.6 us (3%)
    pallas_call x1, Pallas kernels, reduce_all(): pl.pallas_call(functools.partial(reduce_kernel, digits, plan, slab_counts...  142 us
    pallas_call x1, Pallas kernels, gather_all(): pl.pallas_call(functools.partial(gather_kernel, digits, count), out_shape...  142 us
    pallas_call x1, Pallas kernels, ffn(): pl.pallas_call(functools.partial(ffn_kernel, chunk, unrolled), grid=(toke...  70.8 us
    pallas_call x1, Pallas kernels, attend_back(): pl.pallas_call(functools.partial(attend_back_kernel, min(block, tokens),...  41.4 us
    dot_general x6, matrix products, dot_tn(): lax.dot_general(a, b, (((0,), (0,)), ((), ())), preferred_element_type=jn...  39.3 us
    pallas_call x1, Pallas kernels, attend(): pl.pallas_call(functools.partial(attend_kernel, min(block, tokens), head_...  25.5 us
    pallas_call x1, Pallas kernels, project_back(): pl.pallas_call(project_back_kernel, grid=(tokens // rows,), in_specs=[pl....  14.5 us
    pallas_call x1, Pallas kernels, project(): pl.pallas_call(project_kernel, grid=(tokens // rows,), in_specs=[by_row(w...  12.5 us

profile of v2, /device:TPU:0, one launch (start us, length us, event | category | flops | bytes accessed | tf_op | source)
XLA Modules:
  0.0 527.9 jit_solution(3286860975083899410)
XLA Ops:
  0.7 1.8 convert_element_type.62.refs_2_
  2.5 1.8 convert_element_type.63.refs_3_
  4.3 1.7 convert_element_type.60.refs_0_
  6.0 0.0 copy-done.6
  6.0 0.6 convert_element_type.61.refs_1_
  6.7 0.1 reshape.146
  6.7 0.0 copy-done.10
  6.8 0.1 reshape.145
  6.8 0.0 copy-done.13
  6.9 0.7 fusion.28.refs_4_
  7.5 142.1 %gather_all.1 = (bf16[4,2,2,2,32,3072]{5,4,3,2,1,0:T(8,128)(2,1)}, bf16[4,2,2,2,32,1024]{5,4,3,2,1,0:T(8,128)(2,1)}, bf16[4,2,2,2,32,4096]{5,4,3,2,1,0:T(8,128)(...) custom-call(bf16[32,3072]{1,0:T(8,128)(2,1)} %convert_element_type.60.refs_0_, ...), custom_call_target="tpu_custom_call" | custom-call | tf_op jit(solution)/shard_map/gather_all/pallas_call | solution.py:268
  149.7 0.9 copy.40
  150.7 0.1 reshape.171
  150.8 0.7 reshape.167.gain_ref
  151.4 0.1 slice_convert_fusion.1
  151.5 0.1 reshape.172
  151.6 0.7 reshape.168.bias_ref
  152.4 12.5 %project.1 = (bf16[1024,1024]{1,0:T(8,128)(2,1)}, bf16[1024,3072]{1,0:T(8,128)(2,1)}) custom-call(bf16[1024,1024]{1,0:T(8,128)(2,1)} %x_ref.5, bf16[1024,3072]{1,0:T(8,128)(2,1)} %bitcast.78, f32[3,1024]{1,0:T(4,128)} %reshape.167.gain_ref, f32[7,1024]{1,0:T(8,128)} %reshape.168.bias_ref), custom_call_target="tpu_custom_call" | custom-call | tf_op jit(solution)/shard_map/project/pallas_call | solution.py:635
  165.6 0.0 copy-start.9
  165.6 25.5 %attend.1 = (bf16[1024,1024]{1,0:T(8,128)(2,1)}, f32[8,2,1024]{2,1,0:T(2,128)}) custom-call(s32[1]{0:T(128)} %copy.46.len_ref, f32[16]{0:T(128)} %scale_ref.1, bf16[1024,3072]{1,0:T(8,128)(2,1)} %get-tuple-element.40.q_ref.k_ref.v_ref, bf16[1024,3072]{1,0:T(8,128)(2,1)} %get-tuple-element.40.q_ref.k_ref.v_ref, ...), custom_call_target="tpu_custom_call" | custom-call | tf_op jit(solution)/shard_map/attend/pallas_call | solution.py:552
  191.1 0.1 slice_convert_fusion
  191.1 0.6 reshape.173
  191.8 0.7 slice_convert_fusion.2
  192.5 0.1 broadcast_in_dim.22
  192.5 0.7 broadcast_in_dim_reshape.3.scale_ref
  193.2 70.8 %ffn_both.1 = (bf16[1024,1024]{1,0:T(8,128)(2,1)}, bf16[1024,1024]{1,0:T(8,128)(2,1)}, bf16[1024,4096]{1,0:T(8,128)(2,1)}, bf16[1024,4096]{1,0:T(8,128)(2,1)}, b...) custom-call(s32[1]{0:T(128)} %copy.46.len_ref, ...), custom_call_target="tpu_custom_call" | custom-call | tf_op jit(solution)/shard_map/ffn_both/pallas_call | solution.py:492
  264.0 41.4 %attend_back.1 = (bf16[3,1024,1024]{2,1,0:T(8,128)(2,1)}, f32[8,2,1024]{2,1,0:T(2,128)}) custom-call(s32[1]{0:T(128)} %copy.46.len_ref, bf16[1024,3072]{1,0:T(8,128)(2,1)} %get-tuple-element.40.q_ref.k_ref.v_ref, bf16[1024,3072]{1,0:T(8,128)(2,1)} %get-tuple-element.40.q_ref.k_ref.v_ref, bf16[1024,3072]{1,0:T(8,128)(2,1)} %get-tuple-element.40.q_ref.k_ref.v_ref, ...), custom_call_target="tpu_custom_call" | custom-call | tf_op jit(solution)/shard_map/attend_back/pallas_call | solution.py:603
  305.5 0.0 copy-start.4
  305.5 14.5 %project_back.1 = (bf16[1024,1024]{1,0:T(8,128)(2,1)}, f32[4,8,1024]{2,1,0:T(8,128)}) custom-call(bf16[3,1024,1024]{2,1,0:T(8,128)(2,1)} %get-tuple-element.48.d_ref, bf16[1024,1024]{1,0:T(8,128)(2,1)} %x_ref.5, f32[1024,1024]{1,0:T(8,128)} %get-tuple-element.49.dr_ref, bf16[1024,3072]{1,0:T(8,128)(2,1)} %bitcast.79, f32[3,1024]{1,0:T(4,128)} %reshape.167.gain_ref), custom_call_target="tpu_custom_call" | custom-call | tf_op jit(solution)/shard_map/project_back/pallas_call | solution.py:669
  320.0 1.1 reduce_sum.36
  321.1 0.1 reduce_sum.37
  321.2 0.1 reshape.159
  321.3 0.1 copy.31
  321.4 0.1 reshape.160
  321.5 0.1 reshape.157
  321.7 0.1 reshape.158
  321.8 0.1 reduce_sum.39
  321.9 0.1 reshape.163
  322.0 0.1 reduce_sum.38
  322.2 0.1 concatenate.22
  322.3 0.7 copy.37
  323.0 14.7 %convolution_convert_fusion.1 = bf16[1024,4096]{1,0:T(8,128)(2,1)} fusion(bf16[1024,1024]{1,0:T(8,128)(2,1)S(1)} %copy-done.12, bf16[1024,4096]{1,0:T(8,128)(2,1)} %get-tuple-element.54), kind=kOutput, calls=%fused_computation.1 | convolution fusion | flops 8594128896 | bytes 18874368 | tf_op jit(solution)/shard_map/dot_general | solution.py:360
  337.7 4.1 copy.29
  341.8 4.7 fusion.11
  346.6 2.3 fusion.14
  348.9 2.3 fusion.17
  351.3 0.0 slice-start.2
  351.3 6.7 %pad_maximum_fusion.refs_0_ = bf16[4,2,2,2,32,3072]{5,4,3,2,1,0:T(8,128)(2,1)} fusion(bf16[4,2,2,2,32,1024]{5,4,3,2,1,0:T(8,128)(2,1)S(1)} %fusion.17, bf16[4,2,2,2,32,1024]{5,4,3,2,1,0:T(8,128)(2,1)S(1)} %fusion.14, bf16[4,2,2,2,32,1024]{5,4,3,2,1,0:T(8,128)(2,1)S(1)} %fusion.11), kind=kLoop, calls=%fused_computation.2 | loop fusion | flops 18874368 | bytes 12582912 | tf_op jit(solution)/shard_map/concatenate | solution.py:730
  358.0 0.0 copy-start
  358.0 0.0 slice-start.3
  358.0 3.8 convolution_convert_fusion.2
  361.8 0.0 slice-done.3
  361.9 11.4 %convolution_convert_fusion = bf16[4096,1024]{1,0:T(8,128)(2,1)} fusion(bf16[1024,4096]{1,0:T(8,128)(2,1)S(1)} %bitcast.111, bf16[1024,1024]{1,0:T(8,128)(2,1)S(1)} %copy-done, pred[1024]{0:T(1024)(128)(4,1)S(1)} %iota_compare_fusion.1), kind=kOutput, calls=%fused_computation | convolution fusion | flops 8595177472 | bytes 18875392 | tf_op jit(solution)/shard_map/dot_general | solution.py:360
  373.3 142.3 %reduce_all.1 = (f32[32,3072]{1,0:T(8,128)}, f32[32,1024]{1,0:T(8,128)}, f32[32,4096]{1,0:T(8,128)}, f32[128,1024]{1,0:T(8,128)}, f32[8,128]{1,0:T(8,128)}) custom-call(bf16[4,2,2,2,32,3072]{5,4,3,2,1,0:T(8,128)(2,1)} %pad_maximum_fusion.refs_0_, bf16[4,2,2,2,32,1024]{5,4,3,2,1,0:T(8,128)(2,1)} %bitcast.87, bf16[4,2,2,2,32,4096]{5,4,3,2,1,0:T(8,128)(2,1)} %bitcast.82, ...), custom_call_target="tpu_custom_call" | custom-call | tf_op jit(solution)/shard_map/reduce_all/pallas_call | solution.py:323
  515.6 0.8 slice.71
  516.4 0.6 slice.88
  517.0 0.6 slice.87
  517.6 1.3 slice_bitcast_fusion
  518.9 1.3 slice.74
  520.2 1.3 slice.76
  521.4 1.8 copy.47
  523.2 1.6 copy.48
  524.8 1.9 copy.49
  526.7 0.8 copy.50
  (52 shorter events, 0.3 us)
Async XLA Ops:
  0.6 5.4 %copy-start.6 = (f32[32,1024]{1,0:T(8,128)S(1)}, f32[32,1024]{1,0:T(8,128)}, u32[]{:S(2)}) copy-start(f32[32,1024]{1,0:T(8,128)} %param.16) | copy-start | bytes 393220
  0.7 6.0 %copy-start.8 = (f32[7,32]{1,0:T(8,128)S(1)}, f32[7,32]{1,0:T(8,128)}, u32[]{:S(2)}) copy-start(f32[7,32]{1,0:T(8,128)} %param.20) | copy-start | bytes 2692
  0.7 6.1 %copy-start.10 = (f32[3,32]{1,0:T(4,128)S(1)}, f32[3,32]{1,0:T(4,128)}, u32[]{:S(2)}) copy-start(f32[3,32]{1,0:T(4,128)} %param.19) | copy-start | bytes 1156
  0.7 6.2 %copy-start.14 = (f32[128]{0:T(128)S(1)}, f32[128]{0:T(128)}, u32[]{:S(2)}) copy-start(f32[128]{0:T(128)} %param.21) | copy-start | bytes 1540
  0.7 6.2 %copy-start.13 = (f32[2,128]{1,0:T(2,128)S(1)}, f32[2,128]{1,0:T(2,128)}, u32[]{:S(2)}) copy-start(f32[2,128]{1,0:T(2,128)} %param.22) | copy-start | bytes 3076
  165.6 26.9 %copy-start.9 = (f32[16]{0:T(128)S(1)}, f32[16]{0:T(128)}, u32[]{:S(2)}) copy-start(f32[16]{0:T(128)} %scale_ref.1) | copy-start | bytes 196
  305.4 15.7 %copy-start.5 = (f32[7,8,1024]{2,1,0:T(8,128)S(1)}, f32[7,8,1024]{2,1,0:T(8,128)}, u32[]{:S(2)}) copy-start(f32[7,8,1024]{2,1,0:T(8,128)} %get-tuple-element.57) | copy-start | bytes 688132
  305.4 16.3 %copy-start.7 = (f32[8,2,1024]{2,1,0:T(2,128)S(1)}, f32[8,2,1024]{2,1,0:T(2,128)}, u32[]{:S(2)}) copy-start(f32[8,2,1024]{2,1,0:T(2,128)} %get-tuple-element.59) | copy-start | bytes 196612
  305.5 16.5 %copy-start.4 = (f32[3,8,4096]{2,1,0:T(8,128)S(1)}, f32[3,8,4096]{2,1,0:T(8,128)}, u32[]{:S(2)}) copy-start(f32[3,8,4096]{2,1,0:T(8,128)} %get-tuple-element.58) | copy-start | bytes 1179652
  320.0 3.0 copy-start.12
  337.7 8.8 %slice-start = ((s8[6291456]{0:T(1024)(128)(4,1)}), s8[2097152]{0:T(1024)(128)(4,1)S(1)}, s32[]{:S(2)}) async-start(s8[6291456]{0:T(1024)(128)(4,1)} %bitcast.84), calls=%async_computation | async-start | bytes 4194304
  341.8 4.7 slice-start.1
  341.8 4.7 copy-start.2
  351.3 6.7 %copy-start.1 = (bf16[1024,1024]{1,0:T(8,128)(2,1)S(1)}, bf16[1024,1024]{1,0:T(8,128)(2,1)}, u32[]{:S(2)}) copy-start(bf16[1024,1024]{1,0:T(8,128)(2,1)} %get-tuple-element.41.z_ref) | copy-start | bytes 6291460
  351.3 6.7 %copy-start.11 = (bf16[1024,1024]{1,0:T(8,128)(2,1)S(1)}, bf16[1024,1024]{1,0:T(8,128)(2,1)}, u32[]{:S(2)}) copy-start(bf16[1024,1024]{1,0:T(8,128)(2,1)} %get-tuple-element.52) | copy-start | bytes 6291460
  351.3 10.6 %slice-start.2 = ((s8[8388608]{0:T(1024)(128)(4,1)}), s8[4194304]{0:T(1024)(128)(4,1)S(1)}, s32[]{:S(2)}) async-start(s8[8388608]{0:T(1024)(128)(4,1)} %bitcast.110), calls=%async_computation.2 | async-start | bytes 8388608
  358.0 3.8 copy-start
  358.0 3.8 slice-start.3
  515.6 11.1 %copy-start.3 = (f32[128,1024]{1,0:T(8,128)S(1)}, f32[128,1024]{1,0:T(8,128)}, u32[]{:S(2)}) copy-start(f32[128,1024]{1,0:T(8,128)} %get-tuple-element.81) | copy-start | bytes 1572868
